TPU v7x, 32 devices: a whole 2x2x4 slice. The times are simulated.
32 devices in a mesh: grp: 2 (over x), bits: 16 (over z, y, core).
Axes of the slice: x: 2, y: 2, z: 4, core: 2. Of those that a mesh axis runs over, the one named last changes fastest.
Arguments:
- prefix: bfloat16 [128, 16, 1024], P(('grp', 'bits')), parts along dimension 0, may hold values from -6 to 6
- first_suffix: bfloat16 [8, 2, 512, 512], P('grp', None, 'bits'), parts along dimension 0, may hold values from -0.109375 to 0.109375
- pair_prefix: int32 [256, 3], P(('grp', 'bits')), parts along dimension 0, may hold values from 0 to 3
- pair_suffix: int32 [256, 3], P(('grp', 'bits')), parts along dimension 0, may hold values from 0 to 3, all different within a row
- merge_count: int32 [256], P(('grp', 'bits')), parts along dimension 0, may hold values from 1 to 3, as said below
- suffix: bfloat16 [32, 2, 512, 512], P(('grp', 'bits')), parts along dimension 0, may hold values from -0.1875 to 0.1875
- routes: int32 [256, 12], P(('grp', 'bits')), parts along dimension 0, may hold values from 0 to 15, all different within a row; in each aligned block of 8 rows (0 to 7, 8 to 15, ...) at most 8 rows name the same one
- cap: bfloat16 [2, 512, 64], replicated, may hold values from -0.0546875 to 0.0546875
Outputs:
- capped: float32 [256, 16, 128], P(('grp', 'bits')), parts along dimension 0
There are 2 independent parts, one for each index of `grp`. A program takes and returns all parts, laid end to end along the dimension named above; an argument that names none is the same for every part. Nothing has to cross between parts.
Inputs may be any that keep to these rules, and one draw needn't show every extreme that they name: `pair_suffix`: each row names 3 different lifetime-one blocks. `merge_count`: some piece has exactly 3 merges and some exactly one. `routes`: each row names 12 different suffixes; in each aligned block of 8 rows no suffix is named by more than 8 rows, a bound that some block reaches.
All inputs are finite; a program needn't handle non-finite values.
Results may differ from a plain program's by a relative error of at most 0.005.
Values may be sent and summed in bfloat16 or wider, within the bound.
A program may use at most 64 MiB of HBM per device.

v0:
```python
import jax
import jax.numpy as jnp
from jax import lax
from jax.experimental import pallas as pl
from jax.experimental.pallas import tpu as pltpu
from jax.sharding import PartitionSpec as P

HIGHEST_PRECISION = lax.Precision.HIGHEST


def complex_form(blocks):
    real_part = blocks[..., 0, :, :]
    imag_part = blocks[..., 1, :, :]
    upper_half = jnp.concatenate([real_part, imag_part], axis=-1)
    lower_half = jnp.concatenate([-imag_part, real_part], axis=-1)
    return jnp.concatenate([upper_half, lower_half], axis=-2)


def on_device_sparse(prefix, first_suffix, pair_prefix, pair_suffix, merge_count, suffix, routes, cap):
    pieces = pair_prefix.shape[0]
    merges = pair_prefix.shape[1]
    held_blocks = prefix.shape[0]
    rows_piece = prefix.shape[1]
    twice_width = prefix.shape[2]
    half_width = twice_width // 2
    first_count = first_suffix.shape[0]
    listed = routes.shape[1]
    owners = lax.axis_size("bits")
    slot_count = min(pieces, max(2, (2 * pieces * listed + owners - 1) // owners))
    live_mask = lax.broadcasted_iota(jnp.int32, (pieces, merges), 1) < merge_count[:, None]
    matches = (
        pair_suffix[:, :, None] == lax.broadcasted_iota(jnp.int32, (pieces, merges, first_count), 2)
    ) & live_mask[:, :, None]
    which_block = pair_prefix[:, :, None] == lax.broadcasted_iota(
        jnp.int32, (pieces, merges, held_blocks), 2
    )
    prefix_picks = jnp.einsum(
        "ika,ikp->iap", matches.astype(jnp.float32), which_block.astype(jnp.float32)
    ).astype(jnp.bfloat16)
    selected = jnp.einsum(
        "iap,prc->airc", prefix_picks, prefix, preferred_element_type=jnp.float32
    ).astype(jnp.bfloat16)
    selected = selected.reshape(first_count, pieces * rows_piece, twice_width)
    portion = lax.all_gather(first_suffix, "bits", axis=2, tiled=True)
    count_rows = portion.shape[2]
    real_cols = lax.slice_in_dim(selected, 0, count_rows, axis=2)
    imag_cols = lax.dynamic_slice_in_dim(selected, half_width, count_rows, 2)
    left_side = jnp.concatenate([real_cols, imag_cols], axis=2)
    upper_half = jnp.concatenate([portion[:, 0], portion[:, 1]], axis=2)
    lower_half = jnp.concatenate([-portion[:, 1], portion[:, 0]], axis=2)
    right_side = jnp.concatenate([upper_half, lower_half], axis=1)
    state_rows = jnp.einsum(
        "arc,acw->rw", left_side, right_side, preferred_element_type=jnp.float32
    )
    state_rows = state_rows.astype(jnp.bfloat16).reshape(pieces, rows_piece, twice_width)
    named_by = jnp.sum(
        (routes[:, :, None] == lax.broadcasted_iota(jnp.int32, (pieces, listed, owners), 2)).astype(
            jnp.int32
        ),
        axis=1,
    )
    slot_rank = jnp.cumsum(named_by, axis=0) - named_by
    slot_hit = (
        slot_rank[:, :, None] == lax.broadcasted_iota(jnp.int32, (pieces, owners, slot_count), 2)
    ) & (named_by[:, :, None] > 0)
    dispatch = jnp.transpose(slot_hit, (1, 2, 0)).astype(jnp.bfloat16)
    outgoing = jnp.einsum(
        "dmi,irc->dmrc", dispatch, state_rows, preferred_element_type=jnp.float32
    ).astype(jnp.bfloat16)
    own_form = complex_form(suffix[0])
    cap_form = complex_form(cap)
    products = jnp.einsum(
        "smrc,cw->smrw",
        lax.all_to_all(outgoing, "bits", split_axis=0, concat_axis=0, tiled=True),
        own_form,
        preferred_element_type=jnp.float32,
    ).astype(jnp.bfloat16)
    capped_terms = jnp.einsum(
        "smrw,wv->smrv", products, cap_form, preferred_element_type=jnp.float32
    )
    returned = lax.all_to_all(
        capped_terms.astype(jnp.bfloat16), "bits", split_axis=0, concat_axis=0, tiled=True
    ).astype(capped_terms.dtype)
    return jnp.einsum(
        "dmi,dmrv->irv", dispatch.astype(jnp.float32), returned, precision=HIGHEST_PRECISION
    )


def weights_of(pair_prefix, pair_suffix, merge_count, held_blocks, first_count):
    pieces, merges = pair_prefix.shape
    live_mask = lax.broadcasted_iota(jnp.int32, (pieces, merges), 1) < merge_count[:, None]
    matches = (
        pair_suffix[:, :, None] == lax.broadcasted_iota(jnp.int32, (pieces, merges, first_count), 2)
    ) & live_mask[:, :, None]
    which_block = pair_prefix[:, :, None] == lax.broadcasted_iota(
        jnp.int32, (pieces, merges, held_blocks), 2
    )
    return jnp.sum(
        (matches[:, :, :, None] & which_block[:, :, None, :]).astype(jnp.float32), axis=1
    ).astype(jnp.bfloat16)


def on_device_dense(prefix, first_suffix, pair_prefix, pair_suffix, merge_count, suffix, routes, cap):
    pieces = pair_prefix.shape[0]
    held_blocks, rows_piece, twice_width = prefix.shape
    first_count = first_suffix.shape[0]
    owners = lax.axis_size("bits")
    listed = routes.shape[1]
    portion = lax.all_gather(first_suffix, "bits", axis=2, tiled=True)
    cap_form = jnp.concatenate([cap[0], cap[1]], axis=1)
    cap_turn = jnp.concatenate([-cap[1], cap[0]], axis=1)
    closed = (
        jnp.dot(suffix[0, 0], cap_form, preferred_element_type=jnp.float32)
        + jnp.dot(suffix[0, 1], cap_turn, preferred_element_type=jnp.float32)
    ).astype(jnp.bfloat16)
    closed_all = lax.all_gather(closed, "bits", axis=1, tiled=False)
    picks = weights_of(pair_prefix, pair_suffix, merge_count, held_blocks, first_count)
    selected = jnp.einsum(
        "iap,prc->airc", picks, prefix, preferred_element_type=jnp.float32
    ).astype(jnp.bfloat16)
    selected = selected.reshape(first_count, pieces * rows_piece, twice_width)
    half = twice_width // 2
    real = selected[:, :, :half]
    imag = selected[:, :, half:]
    by_real = jnp.einsum(
        "arc,acw->rw", jnp.concatenate([real, -imag], axis=2),
        portion.reshape(first_count, twice_width, half), preferred_element_type=jnp.float32,
    )
    by_imag = jnp.einsum(
        "arc,acw->rw", jnp.concatenate([imag, real], axis=2),
        portion.reshape(first_count, twice_width, half), preferred_element_type=jnp.float32,
    )
    state_real = by_real.astype(jnp.bfloat16)
    state_imag = by_imag.astype(jnp.bfloat16)
    flat = closed_all.reshape(half, -1)
    capw = cap.shape[2]
    stacked = jnp.concatenate([state_real, state_imag], axis=0)
    both = jnp.dot(stacked, flat, preferred_element_type=jnp.float32)
    both = both.reshape(2, pieces, rows_piece, owners, 2, capw)
    named = jnp.sum(
        (routes[:, :, None] == lax.broadcasted_iota(jnp.int32, (pieces, listed, owners), 2)).astype(
            jnp.float32
        ),
        axis=1,
    )
    summed = jnp.sum(both * named[None, :, None, :, None, None], axis=3)
    out_real = summed[0, :, :, 0] - summed[1, :, :, 1]
    out_imag = summed[0, :, :, 1] + summed[1, :, :, 0]
    return jnp.concatenate([out_real, out_imag], axis=-1)


BF = jnp.bfloat16
F32 = jnp.float32


def flip(value, pattern):
    bit = 1
    while bit <= pattern:
        if pattern & bit:
            value = value + bit - 2 * bit * ((value // bit) % 2)
        bit *= 2
    return value


def iota(shape, axis):
    return lax.broadcasted_iota(jnp.int32, shape, axis)


def chain_kernel(
    sizes, x_ref, code_ref, count_ref, route_ref, f_ref, s_ref, cap_ref, out_ref,
    q_ref, qall, fall, mall, sel, tab, pick, name, gall, acc, pair_out, pair_in, ret_out, ret_in,
    q_send, q_recv, f_send, f_recv, m_send, m_recv, p_send, p_recv, r_send, r_recv,
):
    chips, first_count, held, rows_piece, pieces, depth, half, wide = sizes
    rows = pieces * rows_piece
    held_rows = held * rows_piece
    base = first_count * held
    batch = chips // 2
    bundle = min(4, chips)
    me = lax.axis_index("bits")
    core = me % 2
    chip = me // 2
    other = 1 - core
    mate = 2 * chip + other

    def near(pattern):
        return flip(chip, pattern)

    def send(src, dst, send_sem, recv_sem, device):
        return pltpu.make_async_remote_copy(
            src_ref=src, dst_ref=dst, send_sem=send_sem, recv_sem=recv_sem,
            device_id={"bits": device}, device_id_type=pl.DeviceIdType.MESH,
        )

    barrier = pltpu.get_barrier_semaphore()
    pl.semaphore_signal(
        barrier, inc=1, device_id={"bits": mate}, device_id_type=pl.DeviceIdType.MESH
    )
    for t in range(1, chips):
        pl.semaphore_signal(
            barrier, inc=1, device_id={"bits": 2 * near(t) + core},
            device_id_type=pl.DeviceIdType.MESH,
        )

    lane = iota((1, wide), 1)
    sign = jnp.where(lane < wide // 2, -1.0, 1.0).astype(F32)

    def turn(x):
        return pltpu.roll(x, wide // 2, x.ndim - 1) * sign

    spot = iota((pieces, wide), 1)
    table = jnp.zeros((pieces, wide), F32)
    for k in range(code_ref.shape[1]):
        hit = (spot == code_ref[:, k:k + 1]) & (count_ref[...] > k)
        table = table + jnp.where(hit, 1.0, 0.0)
    for k in range(route_ref.shape[1]):
        table = table + jnp.where(spot == route_ref[:, k:k + 1] + base, 1.0, 0.0)
    table = jnp.concatenate([table, jnp.zeros((16 - pieces, wide), F32)], axis=0)
    x = x_ref[...].astype(F32)
    for c in range(chips):
        at = c * (wide // 2)
        q_ref[c, :held_rows] = jnp.concatenate(
            [x[:, at:at + wide // 2], x[:, half + at:half + at + wide // 2]], axis=1
        ).astype(BF)
        q_ref[c, held_rows:] = table.astype(BF)

    def times_cap(block):
        return lax.dot_general(
            block, cap_ref[...], (((1,), (1,)), ((), ())), preferred_element_type=F32
        )

    mall[chip] = (times_cap(s_ref[0]) + turn(times_cap(s_ref[1]))).astype(BF)
    fall[core] = f_ref[...]
    qall[0, chip] = q_ref[chip]

    for a in range(first_count):
        line = iota((wide, wide), 0) - a * held
        gap = iota((wide, wide), 1) - rows_piece * line
        inside = (gap >= 0) & (gap < rows_piece) & (line >= 0) & (line < held)
        pick[:, a * wide:(a + 1) * wide] = jnp.where(inside, 1.0, 0.0).astype(BF)
    for b in range(2):
        for q in range(batch):
            row = base + 2 * near(2 * q + b) + core
            hit = iota((wide, wide), 0) == row
            name[b, :, q * wide:(q + 1) * wide] = jnp.where(hit, 1.0, 0.0).astype(BF)

    pl.semaphore_wait(barrier, chips)

    def q_direct(t):
        target = near(t)
        return send(
            q_ref.at[target], qall.at[0, chip], q_send.at[t], q_recv.at[0, chip],
            2 * target + core,
        )

    def q_mate():
        return send(q_ref.at[chip], qall.at[1, chip], q_send.at[0], q_recv.at[1, chip], mate)

    def q_pass(t):
        slot = near(t)
        return send(
            qall.at[0, slot], qall.at[1, slot], q_send.at[chips + t], q_recv.at[1, slot], mate
        )

    def f_copy(slot):
        return send(f_ref, fall.at[slot], f_send, f_recv, mate)

    def m_copy(slot, index, target):
        return send(
            mall.at[slot], mall.at[slot], m_send.at[index], m_recv.at[slot], 2 * target + core
        )

    lines = [2 * q for q in range(1, batch)]
    for t in range(1, chips):
        q_direct(t).start()
    q_mate().start()
    m_copy(chip, 1, near(1)).start()
    for t in lines:
        m_copy(chip, t, near(t)).start()
    f_copy(core).start()

    def m_arrived(slot):
        m_copy(slot, 0, near(1)).wait_recv()

    def q_arrived(kind, slot):
        send(
            q_ref.at[chip], qall.at[kind, slot], q_send.at[0], q_recv.at[kind, slot], mate
        ).wait_recv()

    full = first_count * wide
    same = (iota((rows, full), 0) - iota((rows, full), 1)) & (rows_piece - 1)
    same = jnp.where(same == 0, 1.0, 0.0).astype(F32)

    def prepare(kind, group):
        first = group * bundle
        blocks = [qall[kind, first + u] for u in range(bundle)]
        for u, block in enumerate(blocks):
            table = block[held_rows:].astype(F32)[:pieces]
            spread = jnp.broadcast_to(table[:, None, :], (pieces, rows_piece, wide))
            tab[kind, first + u] = spread.reshape(rows, wide).astype(BF)
        spreads = tab[kind, pl.ds(first, bundle)].reshape(bundle * rows, wide)
        chosen = jnp.dot(spreads, pick[...], preferred_element_type=F32)
        for u, block in enumerate(blocks):
            kept = (chosen[u * rows:(u + 1) * rows] * same).astype(BF)
            stacked = jnp.concatenate(
                [kept[:, a * wide:a * wide + held_rows] for a in range(first_count)], axis=0
            )
            picked = jnp.dot(stacked, block[:held_rows], preferred_element_type=F32).astype(BF)
            for a in range(first_count):
                sel[kind, first + u, :, a * wide:(a + 1) * wide] = picked[a * rows:(a + 1) * rows]

    def gather_step(slot, b, q):
        product = jnp.dot(
            fall[...].reshape(4 * first_count * depth, half), mall[slot],
            preferred_element_type=F32,
        ).reshape(2, first_count, 2, depth, wide)
        for c in range(2):
            for a in range(first_count):
                by_real, by_imag = product[c, a, 0], product[c, a, 1]
                at = a * 4 * depth + c * depth
                cols = slice(q * wide, (q + 1) * wide)
                gall[b, at:at + depth, cols] = (by_real + turn(by_imag)).astype(BF)
                gall[b, at + 2 * depth:at + 3 * depth, cols] = (turn(by_real) - by_imag).astype(BF)

    for t in range(1, chips):
        q_arrived(0, near(t))
        q_pass(t).start()
    f_copy(other).wait_recv()
    gather_step(chip, 0, 0)

    def prepare_own(group, carry):
        prepare(0, group)
        return carry

    def prepare_other(group, carry):
        for u in range(bundle):
            q_arrived(1, group * bundle + u)
        prepare(1, group)
        return carry

    groups = chips // bundle
    lax.fori_loop(0, groups, prepare_own, 0)
    for t in lines:
        m_arrived(near(t))
        m_copy(near(t), t + 1, near(1)).start()
        gather_step(near(t), 0, t // 2)
    lax.fori_loop(0, groups, prepare_other, 0)

    def part(kind, group, b):
        first = pl.ds(group * bundle, bundle)
        lines_sel = sel[kind, first].reshape(bundle * rows, full)
        lines_tab = tab[kind, first].reshape(bundle * rows, wide)
        values = jnp.dot(lines_sel, gall[b], preferred_element_type=F32)
        named = jnp.dot(lines_tab, name[b], preferred_element_type=F32)
        values = values * named
        total = values[:, :wide]
        for q in range(1, batch):
            total = total + values[:, q * wide:(q + 1) * wide]
        return total.reshape(bundle, rows, wide)

    for kind in (1, 0):
        def first_half(group, carry):
            acc[kind, pl.ds(group * bundle, bundle)] = part(kind, group, 0)
            return carry

        lax.fori_loop(0, groups, first_half, 0)
    for q in range(batch):
        m_arrived(near(2 * q + 1))
        gather_step(near(2 * q + 1), 1, q)

    def pair_copy(c):
        return send(pair_out.at[c], pair_in.at[c], p_send.at[c], p_recv.at[c], mate)

    def second_other(group, carry):
        first = pl.ds(group * bundle, bundle)
        pair_out[first] = (acc[1, first] + part(1, group, 1)).astype(BF)
        for u in range(bundle):
            pair_copy(group * bundle + u).start()
        return carry

    def second_own(group, carry):
        first = pl.ds(group * bundle, bundle)
        acc[0, first] = acc[0, first] + part(0, group, 1)
        return carry

    lax.fori_loop(0, groups, second_other, 0)
    lax.fori_loop(0, groups, second_own, 0)

    def ret_copy(t):
        target = near(t)
        return send(
            ret_out.at[target], ret_in.at[chip], r_send.at[t], r_recv.at[chip], 2 * target + core
        )

    def ret_arrived(source):
        send(
            ret_out.at[source], ret_in.at[source], r_send.at[0], r_recv.at[source],
            2 * source + core,
        ).wait_recv()

    for t in range(chips - 1, 0, -1):
        target = near(t)
        pair_copy(target).wait_recv()
        ret_out[target] = (acc[0, target] + pair_in[target].astype(F32)).astype(BF)
        ret_copy(t).start()
    pair_copy(chip).wait_recv()
    total = acc[0, chip] + pair_in[chip].astype(F32)
    for t in range(1, chips):
        ret_arrived(near(t))
        total = total + ret_in[near(t)].astype(F32)
    out_ref[...] = total

    q_mate().wait_send()
    f_copy(core).wait_send()
    m_copy(chip, 1, near(1)).wait_send()
    for t in lines:
        m_copy(chip, t, near(t)).wait_send()
        m_copy(near(t), t + 1, near(1)).wait_send()
    for t in range(1, chips):
        q_direct(t).wait_send()
        q_pass(t).wait_send()
        ret_copy(t).wait_send()
    for c in range(chips):
        pair_copy(c).wait_send()


def on_device_chain(prefix, first_suffix, pair_prefix, pair_suffix, merge_count, suffix, routes, cap):
    pieces = pair_prefix.shape[0]
    held, rows_piece, twice_width = prefix.shape
    half = twice_width // 2
    first_count, _, depth, _ = first_suffix.shape
    owners = lax.axis_size("bits")
    chips = owners // 2
    wide = 2 * cap.shape[2]
    rows = pieces * rows_piece
    held_rows = held * rows_piece
    code = pair_suffix * held + pair_prefix
    count = merge_count[:, None]
    caps = cap.transpose(0, 2, 1).reshape(wide, half)
    sizes = (chips, first_count, held, rows_piece, pieces, depth, half, wide)
    batch = chips // 2
    vmem = pl.BlockSpec(memory_space=pltpu.VMEM)
    dma = pltpu.SemaphoreType.DMA
    sent = pltpu.VMEM((chips, rows, wide), BF)
    out = pl.pallas_call(
        lambda *refs: chain_kernel(sizes, *refs),
        name="chain",
        out_shape=jax.ShapeDtypeStruct((rows, wide), F32),
        in_specs=[vmem] * 7,
        out_specs=vmem,
        scratch_shapes=[
            pltpu.VMEM((chips, held_rows + 16, wide), BF),
            pltpu.VMEM((2, chips, held_rows + 16, wide), BF),
            pltpu.VMEM((2, first_count, 2, depth, half), BF),
            pltpu.VMEM((chips, half, wide), BF),
            pltpu.VMEM((2, chips, rows, first_count * wide), BF),
            pltpu.VMEM((2, chips, rows, wide), BF),
            pltpu.VMEM((wide, first_count * wide), BF),
            pltpu.VMEM((2, wide, batch * wide), BF),
            pltpu.VMEM((2, first_count * wide, batch * wide), BF),
            pltpu.VMEM((2, chips, rows, wide), F32),
            sent, sent, sent, sent,
            dma((2 * chips,)), dma((2, chips)), dma, dma, dma((chips,)), dma((chips,)),
            dma((chips,)), dma((chips,)), dma((chips,)), dma((chips,)),
        ],
        compiler_params=pltpu.CompilerParams(collective_id=0, has_side_effects=True),
    )(prefix.reshape(held_rows, twice_width), code, count, routes, first_suffix, suffix[0], caps)
    return out.reshape(pieces, rows_piece, wide)


def on_device(prefix, first_suffix, pair_prefix, pair_suffix, merge_count, suffix, routes, cap):
    pieces = pair_prefix.shape[0]
    listed = routes.shape[1]
    owners = lax.axis_size("bits")
    slots = min(pieces, max(2, (2 * pieces * listed + owners - 1) // owners))
    chips = owners // 2
    held, rows_piece, twice_width = prefix.shape
    wide = 2 * cap.shape[2]
    fits = (
        owners % 4 == 0 and chips & (chips - 1) == 0 and wide == 128 and pieces == 8
        and twice_width == chips * wide and first_suffix.shape[0] * held + owners <= wide
        and suffix.shape[0] == 1 and rows_piece == 16 and first_suffix.shape[2] % 16 == 0
    )
    body = on_device_sparse
    if slots == pieces:
        body = on_device_chain if fits else on_device_dense
    return body(
        prefix, first_suffix, pair_prefix, pair_suffix, merge_count, suffix, routes, cap
    )


def solution(mesh):
    return jax.shard_map(
        on_device,
        mesh=mesh,
        in_specs=(
            P(("grp", "bits"), None, None),
            P("grp", None, "bits", None),
            P(("grp", "bits"), None),
            P(("grp", "bits"), None),
            P(("grp", "bits")),
            P(("grp", "bits"), None, None, None),
            P(("grp", "bits"), None),
            P(),
        ),
        out_specs=P(("grp", "bits"), None, None),
        check_vma=False,
    )
```

profile of v0, /device:TPU:0, one launch (start us, length us, event | category | flops | bytes accessed | tf_op | source)
XLA Modules:
  0.0 44.0 jit_solution(6835302940785427876)
XLA Ops:
  0.0 0.0 copy-start
  0.0 0.7 %copy-done = s32[8,3]{0,1:T(4,128)S(1)} copy-done((s32[8,3]{0,1:T(4,128)S(1)}, s32[8,3]{0,1:T(4,128)}, u32[]{:S(2)}) %copy-start) | copy-done | bytes 120
  0.7 0.0 copy-start.1
  0.7 0.1 copy.10
  0.8 0.6 %copy-done.1 = s32[8,3]{0,1:T(4,128)S(1)} copy-done((s32[8,3]{0,1:T(4,128)S(1)}, s32[8,3]{0,1:T(4,128)}, u32[]{:S(2)}) %copy-start.1) | copy-done | bytes 120
  1.4 0.1 copy.9
  1.4 0.0 copy-start.2
  1.4 0.6 %multiply_add_fusion.refs_1_ = s32[8,3]{1,0:T(8,128)} fusion(s32[8,3]{1,0:T(8,128)S(1)} %copy.10, s32[8,3]{1,0:T(8,128)S(1)} %copy.9), kind=kLoop, calls=%fused_computation | loop fusion | flops 48 | bytes 288 | tf_op jit(solution)/shard_map/add | solution.py:437
  2.0 0.1 copy-done.2
  2.1 0.7 %copy.11.refs_2_ = s32[8,1]{1,0:T(8,128)} copy(s32[8,1]{0,1:T(1,128)S(1)} %bitcast.11) | data formatting | bytes 64 | tf_op jit(solution)/shard_map/broadcast_in_dim | solution.py:438
  2.8 39.7 %chain.1 = f32[128,128]{1,0:T(8,128)} custom-call(bf16[64,1024]{1,0:T(8,128)(2,1)} %bitcast.9, s32[8,3]{1,0:T(8,128)} %multiply_add_fusion.refs_1_, s32[8,1]{1,0:T(8,128)} %copy.11.refs_2_, s32[8,12]{1,0:T(8,128)} %refs_3_.1, bf16[4,2,32,512]{3,2,1,0:T(8,128)(2,1)} %refs_4_.1, bf16[2,512,512]{2,1,0:T(8,128)(2,1)} %bitcast.7, bf16[128,512]{1,0:T(8,128)(2,1)} %bitcast.10), custom_call_target="tpu_custom_call" | custom-call | tf_op jit(solution)/shard_map/chain/pallas_call | solution.py:445
  42.5 1.5 %copy.13 = f32[8,16,128]{2,1,0:T(8,128)} copy(f32[8,16,128]{2,1,0:T(8,128)} %bitcast.8) | data formatting | bytes 131072
Async XLA Ops:
  0.0 0.7 %copy-start = (s32[8,3]{0,1:T(4,128)S(1)}, s32[8,3]{0,1:T(4,128)}, u32[]{:S(2)}) copy-start(s32[8,3]{0,1:T(4,128)} %param.10) | copy-start | bytes 292
  0.7 0.7 %copy-start.1 = (s32[8,3]{0,1:T(4,128)S(1)}, s32[8,3]{0,1:T(4,128)}, u32[]{:S(2)}) copy-start(s32[8,3]{0,1:T(4,128)} %param.11) | copy-start | bytes 292
  1.4 0.7 %copy-start.2 = (s32[8]{0:T(128)S(1)}, s32[8]{0:T(128)}, u32[]{:S(2)}) copy-start(s32[8]{0:T(128)} %param.12) | copy-start | bytes 100
where the time goes:
time: 44.2 us; the launch traced here: 44 us
  Pallas kernels  39.7 us (90%)
  local copies, waits for them, and re-layouts  3.65 us (8%)
  other arithmetic  0.6 us (1%)
    pallas_call x1, Pallas kernels, on_device_chain(): pl.pallas_call(lambda *refs: chain_kernel(sizes, *refs), name='chain', ou...  39.7 us
    unnamed x9, local copies, waits for them, and re-layouts  2.98 us

commit v1 on v0

v1 whole, which is shorter than its diff:
```python
import jax
import jax.numpy as jnp
from jax import lax
from jax.experimental import pallas as pl
from jax.experimental.pallas import tpu as pltpu
from jax.sharding import PartitionSpec as P

HIGHEST_PRECISION = lax.Precision.HIGHEST


def complex_form(blocks):
    real_part = blocks[..., 0, :, :]
    imag_part = blocks[..., 1, :, :]
    upper_half = jnp.concatenate([real_part, imag_part], axis=-1)
    lower_half = jnp.concatenate([-imag_part, real_part], axis=-1)
    return jnp.concatenate([upper_half, lower_half], axis=-2)


def on_device_sparse(prefix, first_suffix, pair_prefix, pair_suffix, merge_count, suffix, routes, cap):
    pieces = pair_prefix.shape[0]
    merges = pair_prefix.shape[1]
    held_blocks = prefix.shape[0]
    rows_piece = prefix.shape[1]
    twice_width = prefix.shape[2]
    half_width = twice_width // 2
    first_count = first_suffix.shape[0]
    listed = routes.shape[1]
    owners = lax.axis_size("bits")
    slot_count = min(pieces, max(2, (2 * pieces * listed + owners - 1) // owners))
    live_mask = lax.broadcasted_iota(jnp.int32, (pieces, merges), 1) < merge_count[:, None]
    matches = (
        pair_suffix[:, :, None] == lax.broadcasted_iota(jnp.int32, (pieces, merges, first_count), 2)
    ) & live_mask[:, :, None]
    which_block = pair_prefix[:, :, None] == lax.broadcasted_iota(
        jnp.int32, (pieces, merges, held_blocks), 2
    )
    prefix_picks = jnp.einsum(
        "ika,ikp->iap", matches.astype(jnp.float32), which_block.astype(jnp.float32)
    ).astype(jnp.bfloat16)
    selected = jnp.einsum(
        "iap,prc->airc", prefix_picks, prefix, preferred_element_type=jnp.float32
    ).astype(jnp.bfloat16)
    selected = selected.reshape(first_count, pieces * rows_piece, twice_width)
    portion = lax.all_gather(first_suffix, "bits", axis=2, tiled=True)
    count_rows = portion.shape[2]
    real_cols = lax.slice_in_dim(selected, 0, count_rows, axis=2)
    imag_cols = lax.dynamic_slice_in_dim(selected, half_width, count_rows, 2)
    left_side = jnp.concatenate([real_cols, imag_cols], axis=2)
    upper_half = jnp.concatenate([portion[:, 0], portion[:, 1]], axis=2)
    lower_half = jnp.concatenate([-portion[:, 1], portion[:, 0]], axis=2)
    right_side = jnp.concatenate([upper_half, lower_half], axis=1)
    state_rows = jnp.einsum(
        "arc,acw->rw", left_side, right_side, preferred_element_type=jnp.float32
    )
    state_rows = state_rows.astype(jnp.bfloat16).reshape(pieces, rows_piece, twice_width)
    named_by = jnp.sum(
        (routes[:, :, None] == lax.broadcasted_iota(jnp.int32, (pieces, listed, owners), 2)).astype(
            jnp.int32
        ),
        axis=1,
    )
    earlier = lax.broadcasted_iota(jnp.int32, (pieces, pieces), 0) > lax.broadcasted_iota(
        jnp.int32, (pieces, pieces), 1
    )
    slot_rank = jnp.einsum(
        "ij,jd->id", earlier.astype(jnp.float32), named_by.astype(jnp.float32),
        precision=HIGHEST_PRECISION,
    ).astype(jnp.int32)
    slot_hit = (
        slot_rank[:, :, None] == lax.broadcasted_iota(jnp.int32, (pieces, owners, slot_count), 2)
    ) & (named_by[:, :, None] > 0)
    dispatch = jnp.transpose(slot_hit, (1, 2, 0)).astype(jnp.bfloat16)
    outgoing = jnp.einsum(
        "dmi,irc->dmrc", dispatch, state_rows, preferred_element_type=jnp.float32
    ).astype(jnp.bfloat16)
    own_form = complex_form(suffix[0])
    cap_form = complex_form(cap)
    products = jnp.einsum(
        "smrc,cw->smrw",
        lax.all_to_all(outgoing, "bits", split_axis=0, concat_axis=0, tiled=True),
        own_form,
        preferred_element_type=jnp.float32,
    ).astype(jnp.bfloat16)
    capped_terms = jnp.einsum(
        "smrw,wv->smrv", products, cap_form, preferred_element_type=jnp.float32
    )
    returned = lax.all_to_all(
        capped_terms.astype(jnp.bfloat16), "bits", split_axis=0, concat_axis=0, tiled=True
    ).astype(capped_terms.dtype)
    return jnp.einsum(
        "dmi,dmrv->irv", dispatch.astype(jnp.float32), returned, precision=HIGHEST_PRECISION
    )


def weights_of(pair_prefix, pair_suffix, merge_count, held_blocks, first_count):
    pieces, merges = pair_prefix.shape
    live_mask = lax.broadcasted_iota(jnp.int32, (pieces, merges), 1) < merge_count[:, None]
    matches = (
        pair_suffix[:, :, None] == lax.broadcasted_iota(jnp.int32, (pieces, merges, first_count), 2)
    ) & live_mask[:, :, None]
    which_block = pair_prefix[:, :, None] == lax.broadcasted_iota(
        jnp.int32, (pieces, merges, held_blocks), 2
    )
    return jnp.sum(
        (matches[:, :, :, None] & which_block[:, :, None, :]).astype(jnp.float32), axis=1
    ).astype(jnp.bfloat16)


def on_device_dense(prefix, first_suffix, pair_prefix, pair_suffix, merge_count, suffix, routes, cap):
    pieces = pair_prefix.shape[0]
    held_blocks, rows_piece, twice_width = prefix.shape
    first_count = first_suffix.shape[0]
    owners = lax.axis_size("bits")
    listed = routes.shape[1]
    portion = lax.all_gather(first_suffix, "bits", axis=2, tiled=True)
    cap_form = jnp.concatenate([cap[0], cap[1]], axis=1)
    cap_turn = jnp.concatenate([-cap[1], cap[0]], axis=1)
    closed = (
        jnp.dot(suffix[0, 0], cap_form, preferred_element_type=jnp.float32)
        + jnp.dot(suffix[0, 1], cap_turn, preferred_element_type=jnp.float32)
    ).astype(jnp.bfloat16)
    closed_all = lax.all_gather(closed, "bits", axis=1, tiled=False)
    picks = weights_of(pair_prefix, pair_suffix, merge_count, held_blocks, first_count)
    selected = jnp.einsum(
        "iap,prc->airc", picks, prefix, preferred_element_type=jnp.float32
    ).astype(jnp.bfloat16)
    selected = selected.reshape(first_count, pieces * rows_piece, twice_width)
    half = twice_width // 2
    real = selected[:, :, :half]
    imag = selected[:, :, half:]
    by_real = jnp.einsum(
        "arc,acw->rw", jnp.concatenate([real, -imag], axis=2),
        portion.reshape(first_count, twice_width, half), preferred_element_type=jnp.float32,
    )
    by_imag = jnp.einsum(
        "arc,acw->rw", jnp.concatenate([imag, real], axis=2),
        portion.reshape(first_count, twice_width, half), preferred_element_type=jnp.float32,
    )
    state_real = by_real.astype(jnp.bfloat16)
    state_imag = by_imag.astype(jnp.bfloat16)
    flat = closed_all.reshape(half, -1)
    capw = cap.shape[2]
    stacked = jnp.concatenate([state_real, state_imag], axis=0)
    both = jnp.dot(stacked, flat, preferred_element_type=jnp.float32)
    both = both.reshape(2, pieces, rows_piece, owners, 2, capw)
    named = jnp.sum(
        (routes[:, :, None] == lax.broadcasted_iota(jnp.int32, (pieces, listed, owners), 2)).astype(
            jnp.float32
        ),
        axis=1,
    )
    summed = jnp.sum(both * named[None, :, None, :, None, None], axis=3)
    out_real = summed[0, :, :, 0] - summed[1, :, :, 1]
    out_imag = summed[0, :, :, 1] + summed[1, :, :, 0]
    return jnp.concatenate([out_real, out_imag], axis=-1)


BF = jnp.bfloat16
F32 = jnp.float32


def flip(value, pattern):
    bit = 1
    while bit <= pattern:
        if pattern & bit:
            value = value + bit - 2 * bit * ((value // bit) % 2)
        bit *= 2
    return value


def iota(shape, axis):
    return lax.broadcasted_iota(jnp.int32, shape, axis)


PLANES = 4


def both_parts(real, imag, lanes):
    count = real.shape[0] // 16
    stacked = jnp.stack(
        [real.reshape(count, 16, lanes), imag.reshape(count, 16, lanes)], axis=1
    )
    return stacked.reshape(2 * real.shape[0], lanes)


def planes_kernel(
    sizes, x_ref, pp_ref, ps_ref, count_ref, route_ref, f_hbm, s_hbm, cap_ref, out_ref,
    s_ref, qsend, qall, fall, mt, mall, sel, xy, expand, masks, gall, acc, place, ret_out, ret_in,
    local, q_send, q_recv, q_bulk, f_send, f_recv, m_send, m_recv, r_send, r_recv,
):
    first_count, held, rows_piece, pieces, depth, half, wide = sizes
    rows = pieces * rows_piece
    held_rows = held * rows_piece
    span = half // PLANES
    base = first_count * held
    two = 2 * wide
    me = lax.axis_index("bits")
    z = me // 4
    j = me % 4
    y = j // 2
    middle = (z == 1) | (z == 2)

    def near(pattern):
        return flip(z, pattern)

    def beside(pattern):
        return flip(j, pattern)

    def send(src, dst, send_sem, recv_sem, plane, seat):
        return pltpu.make_async_remote_copy(
            src_ref=src, dst_ref=dst, send_sem=send_sem, recv_sem=recv_sem,
            device_id={"bits": 4 * plane + seat}, device_id_type=pl.DeviceIdType.MESH,
        )

    barrier = pltpu.get_barrier_semaphore()
    for p in range(PLANES):
        for s in range(4):
            if p or s:
                pl.semaphore_signal(
                    barrier, inc=1, device_id={"bits": 4 * near(p) + beside(s)},
                    device_id_type=pl.DeviceIdType.MESH,
                )
    s_copy = pltpu.make_async_copy(s_hbm, s_ref, local.at[0])
    s_copy.start()
    f_local = pltpu.make_async_copy(f_hbm, fall.at[:, :, j], local.at[1])
    f_local.start()

    eye = iota((pieces, pieces), 0) == iota((pieces, pieces), 1)

    def column(row):
        spread = jnp.broadcast_to(row, (pieces, pieces))
        return jnp.sum(jnp.where(eye, spread, 0), axis=1, keepdims=True)

    spot = iota((pieces, wide), 1)
    count = column(count_ref[...])
    table = jnp.zeros((pieces, wide), F32)
    for k in range(pp_ref.shape[0]):
        code = column(ps_ref[k:k + 1, :]) * held + column(pp_ref[k:k + 1, :])
        table = table + jnp.where((spot == code) & (count > k), 1.0, 0.0)
    for k in range(route_ref.shape[1]):
        table = table + jnp.where(spot == route_ref[:, k:k + 1] + base, 1.0, 0.0)
    table = jnp.concatenate([table, jnp.zeros((16 - pieces, wide), F32)], axis=0).astype(BF)
    for p in range(PLANES):
        qsend[p, :held_rows, :wide] = x_ref[:, p * span:(p + 1) * span]
        qsend[p, :held_rows, wide:] = x_ref[:, half + p * span:half + (p + 1) * span]
        qsend[p, held_rows:, :wide] = table
        qsend[p, held_rows:, wide:] = jnp.zeros((16, wide), BF)
    qall[j, z] = qsend[z]

    line = iota((wide, two), 0)
    xy[:, :two] = jnp.where(iota((wide, two), 1) // rows_piece == line, 1.0, 0.0).astype(BF)
    reach = PLANES * wide
    line = iota((wide, reach), 0)
    xy[:, two:] = jnp.where(iota((wide, reach), 1) // 32 + base == line, 1.0, 0.0).astype(BF)
    for q in range(4):
        lane = iota((wide, reach), 0)
        col = iota((wide, reach), 1)
        inside = lane % 32
        goal = (lane // 32) * wide + (inside // 16) * (wide // 2) + 16 * q + inside % 16
        place[q * wide:(q + 1) * wide, :] = jnp.where(col == goal, 1.0, 0.0).astype(BF)

    s_copy.wait()

    def times(left, part):
        return lax.dot_general(
            left, s_ref[part], (((1,), (1,)), ((), ())), preferred_element_type=F32
        )

    upper = both_parts(cap_ref[0], cap_ref[1], half)
    lower = both_parts(-cap_ref[1], cap_ref[0], half)
    closed = (times(upper, 0) + times(lower, 1)).astype(BF)
    mt[...] = closed.reshape(4, 32, half)
    mall[z, j] = mt[j]

    def m_near(t, s):
        return send(
            mt.at[beside(s)], mall.at[z, j], m_send.at[0, t, s], m_recv.at[z, y], near(t),
            beside(s),
        )

    def m_quad(s):
        side = flip(y, 1) if False else y
        return send(
            mt.at[beside(s)], mall.at[z, j], m_send.at[0, 0, s], m_recv.at[z, side], z, beside(s)
        )

    def m_pair(source, side, t, index):
        block = mall.at[source, pl.ds(2 * side, 2)]
        return send(
            block, block, m_send.at[1, t, index], m_recv.at[source, side], near(t), j
        )

    def m_arrived(source, side):
        block = mall.at[source, pl.ds(2 * side, 2)]
        send(block, block, m_send.at[0, 0, 0], m_recv.at[source, side], z, beside(1)).wait_recv()

    def q_line(t):
        return send(
            qsend.at[near(t)], qall.at[j, z], q_send.at[0, t], q_recv.at[j, z], near(t), j
        )

    def q_across(p):
        return send(
            qall.at[j, p], qall.at[j, p], q_send.at[1, p], q_recv.at[j, p], z, beside(2)
        )

    def q_core(s, index):
        return send(
            qall.at[beside(s)], qall.at[beside(s)], q_send.at[2, index], q_bulk.at[beside(s)], z,
            beside(1),
        )

    def q_arrived(seat, plane):
        block = qall.at[seat, plane]
        send(block, block, q_send.at[0, 0], q_recv.at[seat, plane], z, beside(1)).wait_recv()

    def q_bulk_arrived(seat):
        block = qall.at[seat]
        send(block, block, q_send.at[0, 0], q_bulk.at[seat], z, beside(1)).wait_recv()

    def f_copy(s):
        return send(f_hbm, fall.at[:, :, j], f_send.at[s], f_recv.at[j], z, beside(s))

    def f_pass():
        seat = beside(2)
        block = fall.at[:, :, seat]
        return send(block, block, f_send.at[0], f_recv.at[seat], z, beside(1))

    def f_arrived(seat):
        block = fall.at[:, :, seat]
        send(block, block, f_send.at[0], f_recv.at[seat], z, beside(1)).wait_recv()

    same = jnp.where(
        iota((rows_piece, two), 0) == iota((rows_piece, two), 1) % rows_piece, 1.0, 0.0
    ).astype(F32)

    def prepare(seat):
        tabs = jnp.concatenate(
            [qall[seat, p, held_rows:, :wide] for p in range(PLANES)], axis=0
        )
        spread = jnp.dot(tabs, xy[...], preferred_element_type=F32)
        expand[...] = spread[:, :two].reshape(PLANES, 16, two)
        for p in range(PLANES):
            part = spread[:, two + p * wide:two + (p + 1) * wide]
            masks[p, seat] = part.reshape(PLANES, 16, wide)[:, :pieces]

        def one(p, carry):
            wanted = expand[p][:pieces]
            kept = jnp.broadcast_to(wanted[:, None, :], (pieces, rows_piece, two)) * same[None]
            kept = kept.reshape(rows, two)
            group = iota((rows, two), 1) // held_rows
            left = jnp.concatenate(
                [jnp.where(group == a, kept, 0.0).astype(BF) for a in range(first_count)], axis=0
            )
            right = jnp.concatenate([qall[seat, p, :held_rows]] * first_count, axis=0)
            picked = jnp.dot(left, right, preferred_element_type=F32).astype(BF)
            for a in range(first_count):
                sel[seat, p, :, a * two:(a + 1) * two] = picked[a * rows:(a + 1) * rows]
            return carry

        lax.fori_loop(0, PLANES, one, 0)

    def gather(b, planes):
        left = jnp.concatenate([mall[p].reshape(wide, half) for p in planes], axis=0)
        for a in range(first_count):
            product = lax.dot_general(
                left, fall[a].reshape(two, half), (((1,), (1,)), ((), ())),
                preferred_element_type=F32,
            ).reshape(len(planes) * 4, 2, 16, two)
            real = product[:, 0, :, :wide] - product[:, 1, :, wide:]
            imag = product[:, 0, :, wide:] + product[:, 1, :, :wide]
            joined = jnp.stack(
                [jnp.concatenate([real, -imag], axis=-1), jnp.concatenate([imag, real], axis=-1)],
                axis=1,
            )
            gall[b, :, a * two:(a + 1) * two] = joined.reshape(len(planes) * wide, two).astype(BF)

    def part(b, planes, seat):
        lines = sel[seat].reshape(PLANES * rows, first_count * two)
        values = lax.dot_general(
            lines, gall[b], (((1,), (1,)), ((), ())), preferred_element_type=F32
        )
        total = None
        for u, p in enumerate(planes):
            mask = masks[p, seat].reshape(PLANES * pieces, 1, wide)
            mask = jnp.broadcast_to(mask, (PLANES * pieces, rows_piece, wide))
            term = values[:, u * wide:(u + 1) * wide] * mask.reshape(PLANES * rows, wide)
            total = term if total is None else total + term
        return total

    pl.semaphore_wait(barrier, 4 * PLANES - 1)
    for s in (2, 3, 1):
        m_quad(s).start()
    for s in (0, 1):
        for t in (2, 1):
            m_near(t, s).start()

    @pl.when(middle)
    def _():
        for s in (0, 1):
            m_near(3, s).start()

    for t in (3, 2, 1):
        q_line(t).start()
    q_across(z).start()
    for s in (2, 1):
        f_copy(s).start()

    m_arrived(z, flip(y, 1))
    for t in (2, 1):
        m_pair(z, flip(y, 1), t, 0).start()

    @pl.when(middle)
    def _():
        m_pair(z, flip(y, 1), 3, 0).start()

    for t in (1, 2, 3):
        q_arrived(j, near(t))
        q_across(near(t)).start()
    q_core(0, 0).start()

    @pl.when(middle)
    def _():
        m_arrived(near(2), y)
        m_pair(near(2), y, 1, 1).start()

    prepare(j)
    for t in (0, 1, 2, 3):
        q_arrived(beside(2), near(t))
    q_core(2, 1).start()

    @pl.when(middle)
    def _():
        m_arrived(near(2), flip(y, 1))
        m_pair(near(2), flip(y, 1), 1, 2).start()

    prepare(beside(2))
    f_arrived(beside(2))
    f_pass().start()
    for s in (1, 3):
        q_bulk_arrived(beside(s))
        prepare(beside(s))
    send(
        mt.at[j], mall.at[z, beside(1)], m_send.at[0, 0, 0], m_recv.at[z, y], z, beside(1)
    ).wait_recv()
    f_local.wait()
    f_arrived(beside(1))
    f_arrived(beside(3))
    m_arrived(near(1), y)
    m_arrived(near(1), flip(y, 1))
    early = (z, near(1))
    gather(0, early)

    def first_half(seat, carry):
        acc[seat] = part(0, early, seat)
        return carry

    lax.fori_loop(0, 4, first_half, 0)

    @pl.when(jnp.logical_not(middle))
    def _():
        m_arrived(near(2), y)
        m_arrived(near(2), flip(y, 1))

    m_arrived(near(3), y)
    m_arrived(near(3), flip(y, 1))
    late = (near(2), near(3))
    gather(1, late)

    def ret_copy(t, s):
        return send(
            ret_out.at[beside(s), near(t)], ret_in.at[j, z], r_send.at[s, t], r_recv.at[j, z],
            near(t), beside(s),
        )

    group = iota((32, wide), 1) // 32
    for s in (3, 2, 1, 0):
        seat = beside(s)
        total = acc[seat] + part(1, late, seat)
        total = total + pltpu.roll(total, wide // 2, 1)
        total = total + pltpu.roll(total, wide // 4, 1)
        total = total.reshape(PLANES, 4, 32, wide)
        packed = total[:, 3]
        for b in (2, 1, 0):
            packed = jnp.where(group == b, total[:, b], packed)
        ret_out[seat] = packed.astype(BF)
        for t in (3, 2, 1, 0):
            if s or t:
                ret_copy(t, s).start()
    ret_in[j, z] = ret_out[j, z]
    for s in (0, 1, 2, 3):
        for t in range(PLANES):
            if s or t:
                block = ret_in.at[beside(s), near(t)]
                send(
                    block, block, r_send.at[0, 0], r_recv.at[beside(s), near(t)], z, beside(1)
                ).wait_recv()
    left = jnp.concatenate([ret_in[q].reshape(wide, wide) for q in range(4)], axis=1)
    placed = jnp.dot(left, place[...], preferred_element_type=F32).reshape(PLANES, 32, reach)
    summed = jnp.sum(placed, axis=0)
    for b in range(4):
        out_ref[b * 32:(b + 1) * 32] = summed[:, b * wide:(b + 1) * wide]

    for s in (2, 3, 1):
        m_quad(s).wait_send()
    for s in (0, 1):
        for t in (2, 1):
            m_near(t, s).wait_send()
    for t in (2, 1):
        m_pair(z, flip(y, 1), t, 0).wait_send()

    @pl.when(middle)
    def _():
        for s in (0, 1):
            m_near(3, s).wait_send()
        m_pair(z, flip(y, 1), 3, 0).wait_send()
        m_pair(near(2), y, 1, 1).wait_send()
        m_pair(near(2), flip(y, 1), 1, 2).wait_send()

    for t in (3, 2, 1):
        q_line(t).wait_send()
    for p in range(PLANES):
        q_across(near(p)).wait_send()
    q_core(0, 0).wait_send()
    q_core(2, 1).wait_send()
    for s in (2, 1):
        f_copy(s).wait_send()
    f_pass().wait_send()
    for s in range(4):
        for t in range(PLANES):
            if s or t:
                ret_copy(t, s).wait_send()


def on_device_planes(prefix, first_suffix, pair_prefix, pair_suffix, merge_count, suffix, routes, cap):
    pieces = pair_prefix.shape[0]
    held, rows_piece, twice_width = prefix.shape
    half = twice_width // 2
    first_count, _, depth, _ = first_suffix.shape
    wide = 2 * cap.shape[2]
    rows = pieces * rows_piece
    held_rows = held * rows_piece
    two = 2 * wide
    sizes = (first_count, held, rows_piece, pieces, depth, half, wide)
    vmem = pl.BlockSpec(memory_space=pltpu.VMEM)
    hbm = pl.BlockSpec(memory_space=pl.ANY)
    dma = pltpu.SemaphoreType.DMA
    out = pl.pallas_call(
        lambda *refs: planes_kernel(sizes, *refs),
        name="planes",
        out_shape=jax.ShapeDtypeStruct((rows, wide), F32),
        in_specs=[vmem, vmem, vmem, vmem, vmem, hbm, hbm, vmem],
        out_specs=vmem,
        scratch_shapes=[
            pltpu.VMEM((2, half, half), BF),
            pltpu.VMEM((PLANES, held_rows + 16, two), BF),
            pltpu.VMEM((4, PLANES, held_rows + 16, two), BF),
            pltpu.VMEM((first_count, 2, 4, depth, half), BF),
            pltpu.VMEM((4, 32, half), BF),
            pltpu.VMEM((PLANES, 4, 32, half), BF),
            pltpu.VMEM((4, PLANES, rows, first_count * two), BF),
            pltpu.VMEM((wide, two + PLANES * wide), BF),
            pltpu.VMEM((PLANES, 16, two), F32),
            pltpu.VMEM((PLANES, 4, PLANES, pieces, wide), F32),
            pltpu.VMEM((2, two, first_count * two), BF),
            pltpu.VMEM((4, PLANES * rows, wide), F32),
            pltpu.VMEM((4 * wide, PLANES * wide), BF),
            pltpu.VMEM((4, PLANES, 32, wide), BF),
            pltpu.VMEM((4, PLANES, 32, wide), BF),
            dma((2,)), dma((3, 4)), dma((4, PLANES)), dma((4,)), dma((3,)), dma((4,)),
            dma((2, PLANES, 4)), dma((PLANES, 2)), dma((4, PLANES)), dma((4, PLANES)),
        ],
        compiler_params=pltpu.CompilerParams(
            collective_id=0, has_side_effects=True, vmem_limit_bytes=40 * 2 ** 20
        ),
    )(
        prefix.reshape(held_rows, twice_width), pair_prefix.T, pair_suffix.T, merge_count[None],
        routes, first_suffix, suffix[0], cap.transpose(0, 2, 1),
    )
    return out.reshape(pieces, rows_piece, wide)


def on_device(prefix, first_suffix, pair_prefix, pair_suffix, merge_count, suffix, routes, cap):
    pieces = pair_prefix.shape[0]
    listed = routes.shape[1]
    owners = lax.axis_size("bits")
    slots = min(pieces, max(2, (2 * pieces * listed + owners - 1) // owners))
    held, rows_piece, twice_width = prefix.shape
    wide = 2 * cap.shape[2]
    fits = (
        owners == 4 * PLANES and wide == 128 and pieces == 8 and rows_piece == 16
        and twice_width == 2 * PLANES * wide and first_suffix.shape[0] * held == rows_piece
        and held * rows_piece * first_suffix.shape[0] == 2 * wide and suffix.shape[0] == 1
        and owners * first_suffix.shape[2] == twice_width // 2 and owners <= wide - rows_piece
    )
    body = on_device_sparse
    if slots == pieces:
        body = on_device_planes if fits else on_device_dense
    return body(
        prefix, first_suffix, pair_prefix, pair_suffix, merge_count, suffix, routes, cap
    )


def solution(mesh):
    return jax.shard_map(
        on_device,
        mesh=mesh,
        in_specs=(
            P(("grp", "bits"), None, None),
            P("grp", None, "bits", None),
            P(("grp", "bits"), None),
            P(("grp", "bits"), None),
            P(("grp", "bits")),
            P(("grp", "bits"), None, None, None),
            P(("grp", "bits"), None),
            P(),
        ),
        out_specs=P(("grp", "bits"), None, None),
        check_vma=False,
    )
```

time: 44.2 us -> 40.7 us (0.921)
  Pallas kernels: 39.7 us -> 35.1 us
  local copies, waits for them, and re-layouts: 3.65 us -> 5.33 us
  other arithmetic: 0.6 us -> 0 us
    pallas_call x1, Pallas kernels: 39.7 us -> 35.1 us  [on_device_planes(): pl.pallas_call(lambda *refs: planes_kernel(sizes, *refs), name='planes',...]
    unnamed x9 -> x17, local copies, waits for them, and re-layouts: 2.98 us -> 5.33 us
    broadcast_in_dim x1 -> x0, local copies, waits for them, and re-layouts: 0.67 us -> none  [on_device_chain(): count = merge_count[:, None]]
    add x1 -> x0, other arithmetic: 0.6 us -> none  [on_device_chain(): code = pair_suffix * held + pair_prefix]
where the time goes in v1:
time: 40.7 us; the launch traced here: 40.4 us
  Pallas kernels  35.1 us (86%)
  local copies, waits for them, and re-layouts  5.33 us (13%)
    pallas_call x1, Pallas kernels, on_device_planes(): pl.pallas_call(lambda *refs: planes_kernel(sizes, *refs), name='planes',...  35.1 us
    unnamed x17, local copies, waits for them, and re-layouts  5.33 us

profile of v1, /device:TPU:0, one launch (start us, length us, event | category | flops | bytes accessed | tf_op | source)
XLA Modules:
  0.0 40.4 jit_solution(13507142416314873466)
XLA Ops:
  0.0 0.0 copy-start.6
  0.0 0.0 copy-start.4
  0.0 0.0 copy-start.5
  0.0 0.0 copy-start.7
  0.0 0.7 %copy-done.6 = s32[8,3]{0,1:T(4,128)S(1)} copy-done((s32[8,3]{0,1:T(4,128)S(1)}, s32[8,3]{0,1:T(4,128)}, u32[]{:S(2)}) %copy-start.6) | copy-done | bytes 120
  0.7 0.0 copy-done.4
  0.7 0.0 copy-done.5
  0.7 0.0 copy-done.7
  0.7 0.0 copy-start
  0.7 1.2 %copy-done = bf16[1,2,512,512]{3,2,1,0:T(8,128)(2,1)S(1)} copy-done((bf16[1,2,512,512]{3,2,1,0:T(8,128)(2,1)S(1)}, bf16[1,2,512,512]{3,2,1,0:T(8,128)(2,1)}, u32[]{:S(2)}) %copy-start) | copy-done | bytes 1048600
  1.9 0.0 copy-start.1
  1.9 0.9 %copy-done.1 = bf16[4,2,32,512]{3,2,1,0:T(8,128)(2,1)S(1)} copy-done((bf16[4,2,32,512]{3,2,1,0:T(8,128)(2,1)S(1)}, bf16[4,2,32,512]{3,2,1,0:T(8,128)(2,1)}, u32[]{:S(2)}) %copy-start.1) | copy-done | bytes 262168
  2.9 0.0 copy-start.2
  2.9 0.9 %copy-done.2 = bf16[4,16,1024]{2,1,0:T(8,128)(2,1)S(1)} copy-done((bf16[4,16,1024]{2,1,0:T(8,128)(2,1)S(1)}, bf16[4,16,1024]{2,1,0:T(8,128)(2,1)}, u32[]{:S(2)}) %copy-start.2) | copy-done | bytes 131096
  3.8 0.0 copy-start.3
  3.8 0.9 %copy-done.3 = bf16[2,512,64]{1,2,0:T(8,128)(2,1)S(1)} copy-done((bf16[2,512,64]{1,2,0:T(8,128)(2,1)S(1)}, bf16[2,512,64]{1,2,0:T(8,128)(2,1)}, u32[]{:S(2)}) %copy-start.3) | copy-done | bytes 131096
  4.7 35.1 %planes.1 = f32[128,128]{1,0:T(8,128)S(1)} custom-call(bf16[64,1024]{1,0:T(8,128)(2,1)S(1)} %bitcast.9, s32[3,8]{1,0:T(4,128)S(1)} %bitcast.11, s32[3,8]{1,0:T(4,128)S(1)} %bitcast.12, s32[1,8]{1,0:T(1,128)S(1)} %bitcast.13, s32[8,12]{1,0:T(8,128)S(1)} %copy-done.4, bf16[4,2,32,512]{3,2,1,0:T(8,128)(2,1)S(1)} %copy-done.1, bf16[2,512,512]{2,1,0:T(8,128)(2,1)S(1)} %bitcast.7, ...), custom_call_target="tpu_custom_call" | custom-call | tf_op jit(solution)/shard_map/planes/pallas_call | solution.py:548
  39.8 0.6 %copy.10 = f32[8,16,128]{2,1,0:T(8,128)} copy(f32[8,16,128]{2,1,0:T(8,128)S(1)} %bitcast.8) | data formatting | bytes 131072
Async XLA Ops:
  0.0 0.7 %copy-start.6 = (s32[8,3]{0,1:T(4,128)S(1)}, s32[8,3]{0,1:T(4,128)}, u32[]{:S(2)}) copy-start(s32[8,3]{0,1:T(4,128)} %param.11) | copy-start | bytes 292
  0.0 0.7 %copy-start.4 = (s32[8,12]{1,0:T(8,128)S(1)}, s32[8,12]{1,0:T(8,128)}, u32[]{:S(2)}) copy-start(s32[8,12]{1,0:T(8,128)} %refs_4_.1) | copy-start | bytes 1156
  0.0 0.7 %copy-start.5 = (s32[8,3]{0,1:T(4,128)S(1)}, s32[8,3]{0,1:T(4,128)}, u32[]{:S(2)}) copy-start(s32[8,3]{0,1:T(4,128)} %param.10) | copy-start | bytes 292
  0.0 0.7 %copy-start.7 = (s32[8]{0:T(128)S(1)}, s32[8]{0:T(128)}, u32[]{:S(2)}) copy-start(s32[8]{0:T(128)} %param.12) | copy-start | bytes 100
  0.7 1.2 %copy-start = (bf16[1,2,512,512]{3,2,1,0:T(8,128)(2,1)S(1)}, bf16[1,2,512,512]{3,2,1,0:T(8,128)(2,1)}, u32[]{:S(2)}) copy-start(bf16[1,2,512,512]{3,2,1,0:T(8,128)(2,1)} %param.13) | copy-start | bytes 3145732
  1.9 0.9 %copy-start.1 = (bf16[4,2,32,512]{3,2,1,0:T(8,128)(2,1)S(1)}, bf16[4,2,32,512]{3,2,1,0:T(8,128)(2,1)}, u32[]{:S(2)}) copy-start(bf16[4,2,32,512]{3,2,1,0:T(8,128)(2,1)} %refs_5_.1) | copy-start | bytes 786436
  2.9 0.9 %copy-start.2 = (bf16[4,16,1024]{2,1,0:T(8,128)(2,1)S(1)}, bf16[4,16,1024]{2,1,0:T(8,128)(2,1)}, u32[]{:S(2)}) copy-start(bf16[4,16,1024]{2,1,0:T(8,128)(2,1)} %param.8) | copy-start | bytes 393220
  3.8 0.9 %copy-start.3 = (bf16[2,512,64]{1,2,0:T(8,128)(2,1)S(1)}, bf16[2,512,64]{1,2,0:T(8,128)(2,1)}, u32[]{:S(2)}) copy-start(bf16[2,512,64]{1,2,0:T(8,128)(2,1)} %param.15) | copy-start | bytes 393220

commit v2 on v1

--- a/solution.py
+++ b/solution.py
@@ -184,9 +184,9 @@
 
 
 def planes_kernel(
-    sizes, x_ref, pp_ref, ps_ref, count_ref, route_ref, f_hbm, s_hbm, cap_ref, out_ref,
-    s_ref, qsend, qall, fall, mt, mall, sel, xy, expand, masks, gall, acc, place, ret_out, ret_in,
-    local, q_send, q_recv, q_bulk, f_send, f_recv, m_send, m_recv, r_send, r_recv,
+    sizes, x_hbm, pp_hbm, ps_hbm, count_hbm, route_hbm, f_hbm, s_hbm, cap_hbm, out_ref,
+    x_ref, pp_ref, ps_ref, count_ref, route_ref, cap_ref, s_ref, qsend, qall, fall, mt, mall, sel, xy, masks, gall, acc, place, ret_out, ret_in,
+    local, q_send, q_recv, f_send, f_recv, m_send, m_recv, r_send, r_recv,
 ):
     first_count, held, rows_piece, pieces, depth, half, wide = sizes
     rows = pieces * rows_piece
@@ -220,32 +220,13 @@
                     barrier, inc=1, device_id={"bits": 4 * near(p) + beside(s)},
                     device_id_type=pl.DeviceIdType.MESH,
                 )
-    s_copy = pltpu.make_async_copy(s_hbm, s_ref, local.at[0])
-    s_copy.start()
-    f_local = pltpu.make_async_copy(f_hbm, fall.at[:, :, j], local.at[1])
-    f_local.start()
-
-    eye = iota((pieces, pieces), 0) == iota((pieces, pieces), 1)
-
-    def column(row):
-        spread = jnp.broadcast_to(row, (pieces, pieces))
-        return jnp.sum(jnp.where(eye, spread, 0), axis=1, keepdims=True)
-
-    spot = iota((pieces, wide), 1)
-    count = column(count_ref[...])
-    table = jnp.zeros((pieces, wide), F32)
-    for k in range(pp_ref.shape[0]):
-        code = column(ps_ref[k:k + 1, :]) * held + column(pp_ref[k:k + 1, :])
-        table = table + jnp.where((spot == code) & (count > k), 1.0, 0.0)
-    for k in range(route_ref.shape[1]):
-        table = table + jnp.where(spot == route_ref[:, k:k + 1] + base, 1.0, 0.0)
-    table = jnp.concatenate([table, jnp.zeros((16 - pieces, wide), F32)], axis=0).astype(BF)
-    for p in range(PLANES):
-        qsend[p, :held_rows, :wide] = x_ref[:, p * span:(p + 1) * span]
-        qsend[p, :held_rows, wide:] = x_ref[:, half + p * span:half + (p + 1) * span]
-        qsend[p, held_rows:, :wide] = table
-        qsend[p, held_rows:, wide:] = jnp.zeros((16, wide), BF)
-    qall[j, z] = qsend[z]
+    pairs = (
+        (x_hbm, x_ref), (pp_hbm, pp_ref), (ps_hbm, ps_ref), (count_hbm, count_ref),
+        (route_hbm, route_ref), (cap_hbm, cap_ref), (s_hbm, s_ref), (f_hbm, fall.at[:, :, j]),
+    )
+    loads = [pltpu.make_async_copy(a, b, local.at[i]) for i, (a, b) in enumerate(pairs)]
+    for i in (6, 5, 0, 1, 2, 3, 4, 7):
+        loads[i].start()
 
     line = iota((wide, two), 0)
     xy[:, :two] = jnp.where(iota((wide, two), 1) // rows_piece == line, 1.0, 0.0).astype(BF)
@@ -259,7 +240,32 @@
         goal = (lane // 32) * wide + (inside // 16) * (wide // 2) + 16 * q + inside % 16
         place[q * wide:(q + 1) * wide, :] = jnp.where(col == goal, 1.0, 0.0).astype(BF)
 
-    s_copy.wait()
+    for i in (1, 2, 3, 4, 0):
+        loads[i].wait()
+    eye = iota((pieces, pieces), 0) == iota((pieces, pieces), 1)
+
+    def column(row):
+        spread = jnp.broadcast_to(row, (pieces, pieces))
+        return jnp.sum(jnp.where(eye, spread, 0), axis=1, keepdims=True)
+
+    spot = iota((pieces, wide), 1)
+    count = column(count_ref[...])
+    table = jnp.zeros((pieces, wide), F32)
+    for k in range(pp_ref.shape[0]):
+        code = column(ps_ref[k:k + 1, :]) * held + column(pp_ref[k:k + 1, :])
+        table = table + jnp.where((spot == code) & (count > k), 1.0, 0.0)
+    for k in range(route_ref.shape[1]):
+        table = table + jnp.where(spot == route_ref[:, k:k + 1] + base, 1.0, 0.0)
+    table = table.astype(BF)
+    for p in range(PLANES):
+        qsend[p, :held_rows, :wide] = x_ref[:, p * span:(p + 1) * span]
+        qsend[p, :held_rows, wide:] = x_ref[:, half + p * span:half + (p + 1) * span]
+        qsend[p, held_rows:, :wide] = table
+        qsend[p, held_rows:, wide:] = jnp.zeros((pieces, wide), BF)
+    qall[z, j] = qsend[z]
+
+    loads[5].wait()
+    loads[6].wait()
 
     def times(left, part):
         return lax.dot_general(
@@ -296,27 +302,20 @@
 
     def q_line(t):
         return send(
-            qsend.at[near(t)], qall.at[j, z], q_send.at[0, t], q_recv.at[j, z], near(t), j
-        )
-
-    def q_across(p):
+            qsend.at[near(t)], qall.at[z, j], q_send.at[0, t], q_recv.at[z, j], near(t), j
+        )
+
+    def q_pass(t, s, to):
+        block = qall.at[near(t), beside(s)]
         return send(
-            qall.at[j, p], qall.at[j, p], q_send.at[1, p], q_recv.at[j, p], z, beside(2)
-        )
-
-    def q_core(s, index):
-        return send(
-            qall.at[beside(s)], qall.at[beside(s)], q_send.at[2, index], q_bulk.at[beside(s)], z,
-            beside(1),
-        )
-
-    def q_arrived(seat, plane):
-        block = qall.at[seat, plane]
-        send(block, block, q_send.at[0, 0], q_recv.at[seat, plane], z, beside(1)).wait_recv()
-
-    def q_bulk_arrived(seat):
-        block = qall.at[seat]
-        send(block, block, q_send.at[0, 0], q_bulk.at[seat], z, beside(1)).wait_recv()
+            block, block, q_send.at[to + s // 2, t], q_recv.at[near(t), beside(s)], z, beside(to)
+        )
+
+    def q_arrived(t, s):
+        block = qall.at[near(t), beside(s)]
+        send(
+            block, block, q_send.at[0, 0], q_recv.at[near(t), beside(s)], z, beside(1)
+        ).wait_recv()
 
     def f_copy(s):
         return send(f_hbm, fall.at[:, :, j], f_send.at[s], f_recv.at[j], z, beside(s))
@@ -334,31 +333,28 @@
         iota((rows_piece, two), 0) == iota((rows_piece, two), 1) % rows_piece, 1.0, 0.0
     ).astype(F32)
 
-    def prepare(seat):
+    group_of = iota((rows, two), 1) // held_rows
+
+    def prepare(t):
+        plane = near(t)
         tabs = jnp.concatenate(
-            [qall[seat, p, held_rows:, :wide] for p in range(PLANES)], axis=0
-        )
+            [qall[plane, q, held_rows:, :wide].astype(F32) for q in range(4)], axis=0
+        ).astype(BF)
         spread = jnp.dot(tabs, xy[...], preferred_element_type=F32)
-        expand[...] = spread[:, :two].reshape(PLANES, 16, two)
         for p in range(PLANES):
-            part = spread[:, two + p * wide:two + (p + 1) * wide]
-            masks[p, seat] = part.reshape(PLANES, 16, wide)[:, :pieces]
-
-        def one(p, carry):
-            wanted = expand[p][:pieces]
+            masks[p, plane] = spread[:, two + p * wide:two + (p + 1) * wide]
+        for q in range(4):
+            wanted = spread[q * pieces:(q + 1) * pieces, :two]
             kept = jnp.broadcast_to(wanted[:, None, :], (pieces, rows_piece, two)) * same[None]
             kept = kept.reshape(rows, two)
-            group = iota((rows, two), 1) // held_rows
             left = jnp.concatenate(
-                [jnp.where(group == a, kept, 0.0).astype(BF) for a in range(first_count)], axis=0
+                [jnp.where(group_of == a, kept, 0.0).astype(BF) for a in range(first_count)],
+                axis=0,
             )
-            right = jnp.concatenate([qall[seat, p, :held_rows]] * first_count, axis=0)
+            right = jnp.concatenate([qall[plane, q, :held_rows]] * first_count, axis=0)
             picked = jnp.dot(left, right, preferred_element_type=F32).astype(BF)
             for a in range(first_count):
-                sel[seat, p, :, a * two:(a + 1) * two] = picked[a * rows:(a + 1) * rows]
-            return carry
-
-        lax.fori_loop(0, PLANES, one, 0)
+                sel[plane, q, :, a * two:(a + 1) * two] = picked[a * rows:(a + 1) * rows]
 
     def gather(b, planes):
         left = jnp.concatenate([mall[p].reshape(wide, half) for p in planes], axis=0)
@@ -375,16 +371,16 @@
             )
             gall[b, :, a * two:(a + 1) * two] = joined.reshape(len(planes) * wide, two).astype(BF)
 
-    def part(b, planes, seat):
-        lines = sel[seat].reshape(PLANES * rows, first_count * two)
+    def part(b, planes, owner):
+        lines = sel[owner].reshape(4 * rows, first_count * two)
         values = lax.dot_general(
             lines, gall[b], (((1,), (1,)), ((), ())), preferred_element_type=F32
         )
         total = None
         for u, p in enumerate(planes):
-            mask = masks[p, seat].reshape(PLANES * pieces, 1, wide)
-            mask = jnp.broadcast_to(mask, (PLANES * pieces, rows_piece, wide))
-            term = values[:, u * wide:(u + 1) * wide] * mask.reshape(PLANES * rows, wide)
+            mask = masks[p, owner].reshape(4 * pieces, 1, wide)
+            mask = jnp.broadcast_to(mask, (4 * pieces, rows_piece, wide))
+            term = values[:, u * wide:(u + 1) * wide] * mask.reshape(4 * rows, wide)
             total = term if total is None else total + term
         return total
 
@@ -402,57 +398,84 @@
 
     for t in (3, 2, 1):
         q_line(t).start()
-    q_across(z).start()
+    for to in (2, 1):
+        q_pass(0, 0, to).start()
     for s in (2, 1):
         f_copy(s).start()
-
-    m_arrived(z, flip(y, 1))
-    for t in (2, 1):
-        m_pair(z, flip(y, 1), t, 0).start()
+    far = flip(y, 1)
+
+    q_arrived(0, 2)
+    q_pass(0, 2, 1).start()
+    m_arrived(z, far)
+    m_pair(z, far, 1, 0).start()
 
     @pl.when(middle)
     def _():
-        m_pair(z, flip(y, 1), 3, 0).start()
-
-    for t in (1, 2, 3):
-        q_arrived(j, near(t))
-        q_across(near(t)).start()
-    q_core(0, 0).start()
+        m_pair(z, far, 3, 0).start()
+
+    @pl.when(jnp.logical_not(middle))
+    def _():
+        m_pair(z, far, 2, 0).start()
+
+    def q_spread(t):
+        q_arrived(t, 0)
+        for to in (2, 1):
+            q_pass(t, 0, to).start()
+
+    def q_second(t):
+        q_arrived(t, 2)
+        q_pass(t, 2, 1).start()
+
+    def q_rest(t):
+        q_arrived(t, 1)
+        q_arrived(t, 3)
+
+    q_spread(1)
+    q_rest(0)
+    prepare(0)
+    q_spread(2)
+    q_spread(3)
 
     @pl.when(middle)
     def _():
         m_arrived(near(2), y)
         m_pair(near(2), y, 1, 1).start()
 
-    prepare(j)
-    for t in (0, 1, 2, 3):
-        q_arrived(beside(2), near(t))
-    q_core(2, 1).start()
+    q_second(1)
+    q_rest(1)
+    prepare(1)
 
     @pl.when(middle)
     def _():
-        m_arrived(near(2), flip(y, 1))
-        m_pair(near(2), flip(y, 1), 1, 2).start()
-
-    prepare(beside(2))
+        m_arrived(near(3), far)
+        m_pair(near(3), far, 1, 2).start()
+
+    q_second(2)
+    q_second(3)
+
+    @pl.when(middle)
+    def _():
+        m_arrived(near(2), far)
+        m_pair(near(2), far, 1, 3).start()
+
     f_arrived(beside(2))
     f_pass().start()
-    for s in (1, 3):
-        q_bulk_arrived(beside(s))
-        prepare(beside(s))
+    for t in (2, 3):
+        q_rest(t)
+        prepare(t)
     send(
         mt.at[j], mall.at[z, beside(1)], m_send.at[0, 0, 0], m_recv.at[z, y], z, beside(1)
     ).wait_recv()
-    f_local.wait()
+    loads[7].wait()
     f_arrived(beside(1))
     f_arrived(beside(3))
     m_arrived(near(1), y)
-    m_arrived(near(1), flip(y, 1))
+    m_arrived(near(1), far)
     early = (z, near(1))
     gather(0, early)
 
-    def first_half(seat, carry):
-        acc[seat] = part(0, early, seat)
+    def first_half(owner, carry):
+        acc[owner] = part(0, early, owner)
         return carry
 
     lax.fori_loop(0, 4, first_half, 0)
@@ -460,36 +483,36 @@
     @pl.when(jnp.logical_not(middle))
     def _():
         m_arrived(near(2), y)
-        m_arrived(near(2), flip(y, 1))
+        m_arrived(near(2), far)
+        m_arrived(near(3), far)
 
     m_arrived(near(3), y)
-    m_arrived(near(3), flip(y, 1))
     late = (near(2), near(3))
     gather(1, late)
 
     def ret_copy(t, s):
         return send(
-            ret_out.at[beside(s), near(t)], ret_in.at[j, z], r_send.at[s, t], r_recv.at[j, z],
+            ret_out.at[near(t), beside(s)], ret_in.at[j, z], r_send.at[s, t], r_recv.at[j, z],
             near(t), beside(s),
         )
 
     group = iota((32, wide), 1) // 32
-    for s in (3, 2, 1, 0):
-        seat = beside(s)
-        total = acc[seat] + part(1, late, seat)
+    for t in (3, 2, 1, 0):
+        owner = near(t)
+        total = acc[owner] + part(1, late, owner)
         total = total + pltpu.roll(total, wide // 2, 1)
         total = total + pltpu.roll(total, wide // 4, 1)
-        total = total.reshape(PLANES, 4, 32, wide)
+        total = total.reshape(4, 4, 32, wide)
         packed = total[:, 3]
         for b in (2, 1, 0):
             packed = jnp.where(group == b, total[:, b], packed)
-        ret_out[seat] = packed.astype(BF)
-        for t in (3, 2, 1, 0):
+        ret_out[owner] = packed.astype(BF)
+        for s in (3, 2, 1, 0):
             if s or t:
                 ret_copy(t, s).start()
-    ret_in[j, z] = ret_out[j, z]
-    for s in (0, 1, 2, 3):
-        for t in range(PLANES):
+    ret_in[j, z] = ret_out[z, j]
+    for t in range(PLANES):
+        for s in (0, 1, 2, 3):
             if s or t:
                 block = ret_in.at[beside(s), near(t)]
                 send(
@@ -506,23 +529,27 @@
     for s in (0, 1):
         for t in (2, 1):
             m_near(t, s).wait_send()
-    for t in (2, 1):
-        m_pair(z, flip(y, 1), t, 0).wait_send()
+    m_pair(z, far, 1, 0).wait_send()
 
     @pl.when(middle)
     def _():
         for s in (0, 1):
             m_near(3, s).wait_send()
-        m_pair(z, flip(y, 1), 3, 0).wait_send()
+        m_pair(z, far, 3, 0).wait_send()
         m_pair(near(2), y, 1, 1).wait_send()
-        m_pair(near(2), flip(y, 1), 1, 2).wait_send()
+        m_pair(near(3), far, 1, 2).wait_send()
+        m_pair(near(2), far, 1, 3).wait_send()
+
+    @pl.when(jnp.logical_not(middle))
+    def _():
+        m_pair(z, far, 2, 0).wait_send()
 
     for t in (3, 2, 1):
         q_line(t).wait_send()
-    for p in range(PLANES):
-        q_across(near(p)).wait_send()
-    q_core(0, 0).wait_send()
-    q_core(2, 1).wait_send()
+    for t in range(PLANES):
+        for to in (2, 1):
+            q_pass(t, 0, to).wait_send()
+        q_pass(t, 2, 1).wait_send()
     for s in (2, 1):
         f_copy(s).wait_send()
     f_pass().wait_send()
@@ -543,40 +570,45 @@
     two = 2 * wide
     sizes = (first_count, held, rows_piece, pieces, depth, half, wide)
     vmem = pl.BlockSpec(memory_space=pltpu.VMEM)
-    hbm = pl.BlockSpec(memory_space=pl.ANY)
+    hbm = pl.BlockSpec(memory_space=pltpu.HBM)
     dma = pltpu.SemaphoreType.DMA
     out = pl.pallas_call(
         lambda *refs: planes_kernel(sizes, *refs),
         name="planes",
         out_shape=jax.ShapeDtypeStruct((rows, wide), F32),
-        in_specs=[vmem, vmem, vmem, vmem, vmem, hbm, hbm, vmem],
+        in_specs=[hbm] * 8,
         out_specs=vmem,
         scratch_shapes=[
+            pltpu.VMEM((held_rows, twice_width), BF),
+            pltpu.VMEM(pair_prefix.shape[::-1], jnp.int32),
+            pltpu.VMEM(pair_prefix.shape[::-1], jnp.int32),
+            pltpu.VMEM((1, pieces), jnp.int32),
+            pltpu.VMEM(routes.shape, jnp.int32),
+            pltpu.VMEM((2, wide // 2, half), BF),
             pltpu.VMEM((2, half, half), BF),
-            pltpu.VMEM((PLANES, held_rows + 16, two), BF),
-            pltpu.VMEM((4, PLANES, held_rows + 16, two), BF),
+            pltpu.VMEM((PLANES, held_rows + pieces, two), BF),
+            pltpu.VMEM((PLANES, 4, held_rows + pieces, two), BF),
             pltpu.VMEM((first_count, 2, 4, depth, half), BF),
             pltpu.VMEM((4, 32, half), BF),
             pltpu.VMEM((PLANES, 4, 32, half), BF),
-            pltpu.VMEM((4, PLANES, rows, first_count * two), BF),
+            pltpu.VMEM((PLANES, 4, rows, first_count * two), BF),
             pltpu.VMEM((wide, two + PLANES * wide), BF),
-            pltpu.VMEM((PLANES, 16, two), F32),
-            pltpu.VMEM((PLANES, 4, PLANES, pieces, wide), F32),
+            pltpu.VMEM((PLANES, PLANES, 4 * pieces, wide), F32),
             pltpu.VMEM((2, two, first_count * two), BF),
-            pltpu.VMEM((4, PLANES * rows, wide), F32),
+            pltpu.VMEM((PLANES, 4 * rows, wide), F32),
             pltpu.VMEM((4 * wide, PLANES * wide), BF),
+            pltpu.VMEM((PLANES, 4, 32, wide), BF),
             pltpu.VMEM((4, PLANES, 32, wide), BF),
-            pltpu.VMEM((4, PLANES, 32, wide), BF),
-            dma((2,)), dma((3, 4)), dma((4, PLANES)), dma((4,)), dma((3,)), dma((4,)),
+            dma((8,)), dma((4, PLANES)), dma((PLANES, 4)), dma((3,)), dma((4,)),
             dma((2, PLANES, 4)), dma((PLANES, 2)), dma((4, PLANES)), dma((4, PLANES)),
         ],
         compiler_params=pltpu.CompilerParams(
             collective_id=0, has_side_effects=True, vmem_limit_bytes=40 * 2 ** 20
         ),
-    )(
+    )(*[pltpu.with_memory_space_constraint(v, pltpu.HBM) for v in (
         prefix.reshape(held_rows, twice_width), pair_prefix.T, pair_suffix.T, merge_count[None],
         routes, first_suffix, suffix[0], cap.transpose(0, 2, 1),
-    )
+    )])
     return out.reshape(pieces, rows_piece, wide)
 
 

time: 40.7 us -> 32.4 us (0.80)
  local copies, waits for them, and re-layouts: 5.33 us -> 0.63 us
  Pallas kernels: 35.1 us -> 31.6 us
    unnamed x17 -> x1, local copies, waits for them, and re-layouts: 5.33 us -> 0.63 us
    pallas_call x1, Pallas kernels: 35.1 us -> 31.6 us  [on_device_planes(): pl.pallas_call(lambda *refs: planes_kernel(sizes, *refs), name='planes',...]
where the time goes in v2:
time: 32.4 us; the launch traced here: 32.2 us
  Pallas kernels  31.6 us (98%)
  local copies, waits for them, and re-layouts  0.63 us (2%)
    pallas_call x1, Pallas kernels, on_device_planes(): pl.pallas_call(lambda *refs: planes_kernel(sizes, *refs), name='planes',...  31.6 us

profile of v2, /device:TPU:0, one launch (start us, length us, event | category | flops | bytes accessed | tf_op | source)
XLA Modules:
  0.0 32.2 jit_solution(12121035848543849158)
XLA Ops:
  0.0 31.6 %planes.1 = f32[128,128]{1,0:T(8,128)S(1)} custom-call(bf16[64,1024]{1,0:T(8,128)(2,1)} %bitcast.9, s32[3,8]{1,0:T(4,128)} %bitcast.11, s32[3,8]{1,0:T(4,128)} %bitcast.12, s32[1,8]{1,0:T(1,128)} %bitcast.13, s32[8,12]{1,0:T(8,128)} %refs_4_.1, bf16[4,2,32,512]{3,2,1,0:T(8,128)(2,1)} %refs_5_.1, bf16[2,512,512]{2,1,0:T(8,128)(2,1)} %bitcast.8, ...), custom_call_target="tpu_custom_call" | custom-call | tf_op jit(solution)/shard_map/planes/pallas_call | solution.py:575
  31.6 0.6 %copy.10 = f32[8,16,128]{2,1,0:T(8,128)} copy(f32[8,16,128]{2,1,0:T(8,128)S(1)} %bitcast.7) | data formatting | bytes 131072

commit v3 on v2

--- a/solution.py
+++ b/solution.py
@@ -213,7 +213,7 @@
         )
 
     barrier = pltpu.get_barrier_semaphore()
-    for p in range(PLANES):
+    for p in (1, 2, 3, 0):
         for s in range(4):
             if p or s:
                 pl.semaphore_signal(
@@ -317,17 +317,26 @@
             block, block, q_send.at[0, 0], q_recv.at[near(t), beside(s)], z, beside(1)
         ).wait_recv()
 
-    def f_copy(s):
-        return send(f_hbm, fall.at[:, :, j], f_send.at[s], f_recv.at[j], z, beside(s))
-
-    def f_pass():
-        seat = beside(2)
-        block = fall.at[:, :, seat]
-        return send(block, block, f_send.at[0], f_recv.at[seat], z, beside(1))
-
-    def f_arrived(seat):
-        block = fall.at[:, :, seat]
-        send(block, block, f_send.at[0], f_recv.at[seat], z, beside(1)).wait_recv()
+    cuts = [(0, first_count // 2)] + [(a, 1) for a in range(first_count // 2, first_count)]
+
+    def f_block(i, seat):
+        first, size = cuts[i]
+        return fall.at[pl.ds(first, size), :, seat]
+
+    def f_copy(s, i):
+        first, size = cuts[i]
+        return send(
+            f_hbm.at[pl.ds(first, size)], f_block(i, j), f_send.at[s, i], f_recv.at[j, i], z,
+            beside(s),
+        )
+
+    def f_pass(i):
+        block = f_block(i, beside(2))
+        return send(block, block, f_send.at[0, i], f_recv.at[beside(2), i], z, beside(1))
+
+    def f_arrived(s, i):
+        block = f_block(i, beside(s))
+        send(block, block, f_send.at[0, i], f_recv.at[beside(s), i], z, beside(1)).wait_recv()
 
     same = jnp.where(
         iota((rows_piece, two), 0) == iota((rows_piece, two), 1) % rows_piece, 1.0, 0.0
@@ -357,81 +366,109 @@
                 sel[plane, q, :, a * two:(a + 1) * two] = picked[a * rows:(a + 1) * rows]
 
     def gather(b, planes):
-        left = jnp.concatenate([mall[p].reshape(wide, half) for p in planes], axis=0)
+        caps = jnp.concatenate([mall[p].reshape(wide, half) for p in planes], axis=0)
+        split = caps.reshape(4 * len(planes), 2, 16, half)
+        turned = jnp.stack([-split[:, 1], split[:, 0]], axis=1).reshape(caps.shape)
+        right = jnp.concatenate(
+            [jnp.concatenate([caps, turned], axis=1), jnp.concatenate([turned, -caps], axis=1)],
+            axis=0,
+        )
+        left = jnp.concatenate(
+            [fall[:, r].reshape(first_count * wide, half) for r in range(2)], axis=1
+        )
+        product = lax.dot_general(
+            left, right, (((1,), (1,)), ((), ())), preferred_element_type=F32
+        ).astype(BF)
         for a in range(first_count):
-            product = lax.dot_general(
-                left, fall[a].reshape(two, half), (((1,), (1,)), ((), ())),
-                preferred_element_type=F32,
-            ).reshape(len(planes) * 4, 2, 16, two)
-            real = product[:, 0, :, :wide] - product[:, 1, :, wide:]
-            imag = product[:, 0, :, wide:] + product[:, 1, :, :wide]
-            joined = jnp.stack(
-                [jnp.concatenate([real, -imag], axis=-1), jnp.concatenate([imag, real], axis=-1)],
-                axis=1,
-            )
-            gall[b, :, a * two:(a + 1) * two] = joined.reshape(len(planes) * wide, two).astype(BF)
-
-    def part(b, planes, owner):
-        lines = sel[owner].reshape(4 * rows, first_count * two)
-        values = lax.dot_general(
-            lines, gall[b], (((1,), (1,)), ((), ())), preferred_element_type=F32
-        )
+            for r in range(2):
+                gall[b, a * two + r * wide:a * two + (r + 1) * wide] = product[
+                    a * wide:(a + 1) * wide, r * two:(r + 1) * two
+                ]
+
+    own_pair = pl.ds(2 * (z // 2), 2)
+    other_pair = pl.ds(2 - 2 * (z // 2), 2)
+
+    def part(b, planes, pair):
+        lines = sel[pair].reshape(8 * rows, first_count * two)
+        values = jnp.dot(lines, gall[b], preferred_element_type=F32)
         total = None
         for u, p in enumerate(planes):
-            mask = masks[p, owner].reshape(4 * pieces, 1, wide)
-            mask = jnp.broadcast_to(mask, (4 * pieces, rows_piece, wide))
-            term = values[:, u * wide:(u + 1) * wide] * mask.reshape(4 * rows, wide)
+            mask = masks[p, pair].reshape(8 * pieces, 1, wide)
+            mask = jnp.broadcast_to(mask, (8 * pieces, rows_piece, wide))
+            term = values[:, u * wide:(u + 1) * wide] * mask.reshape(8 * rows, wide)
             total = term if total is None else total + term
-        return total
+        return total.reshape(2, 4 * rows, wide)
 
     pl.semaphore_wait(barrier, 4 * PLANES - 1)
-    for s in (2, 3, 1):
+    far = flip(y, 1)
+    early = (z, near(1))
+
+    def q_spread(t):
+        q_arrived(t, 0)
+        for to in (2, 1):
+            q_pass(t, 0, to).start()
+
+    def q_second(t):
+        q_arrived(t, 2)
+        q_pass(t, 2, 1).start()
+
+    def q_rest(t):
+        q_arrived(t, 1)
+        q_arrived(t, 3)
+
+    def first_half(pair):
+        acc[pair] = part(0, early, pair)
+
+    edge = jnp.logical_not(middle)
+    for s in (2, 3):
         m_quad(s).start()
-    for s in (0, 1):
-        for t in (2, 1):
-            m_near(t, s).start()
-
-    @pl.when(middle)
-    def _():
-        for s in (0, 1):
-            m_near(3, s).start()
-
     for t in (3, 2, 1):
         q_line(t).start()
     for to in (2, 1):
         q_pass(0, 0, to).start()
-    for s in (2, 1):
-        f_copy(s).start()
-    far = flip(y, 1)
-
-    q_arrived(0, 2)
-    q_pass(0, 2, 1).start()
+    m_quad(1).start()
+    q_arrived(0, 1)
+
+    @pl.when(edge)
+    def _():
+        for s in (0, 1):
+            m_near(2, s).start()
+
+    @pl.when(middle)
+    def _():
+        for t in (1, 3):
+            for s in (0, 1):
+                m_near(t, s).start()
+
+    f_copy(2, 0).start()
+    for i in range(len(cuts)):
+        f_copy(1, i).start()
     m_arrived(z, far)
-    m_pair(z, far, 1, 0).start()
 
     @pl.when(middle)
     def _():
-        m_pair(z, far, 3, 0).start()
-
-    @pl.when(jnp.logical_not(middle))
+        for t in (1, 3):
+            m_pair(z, far, t, 0).start()
+
+    @pl.when(edge)
     def _():
         m_pair(z, far, 2, 0).start()
-
-    def q_spread(t):
-        q_arrived(t, 0)
-        for to in (2, 1):
-            q_pass(t, 0, to).start()
-
-    def q_second(t):
-        q_arrived(t, 2)
-        q_pass(t, 2, 1).start()
-
-    def q_rest(t):
-        q_arrived(t, 1)
-        q_arrived(t, 3)
-
+        for s in (0, 1):
+            m_near(1, s).start()
+        m_pair(z, far, 1, 0).start()
+
+    f_copy(2, 1).start()
+    q_second(0)
     q_spread(1)
-    q_rest(0)
+    for i in range(2, len(cuts)):
+        f_copy(2, i).start()
+
+    @pl.when(middle)
+    def _():
+        for s in (0, 1):
+            m_near(2, s).start()
+
+    q_arrived(0, 3)
     prepare(0)
     q_spread(2)
     q_spread(3)
@@ -442,43 +479,39 @@
         m_pair(near(2), y, 1, 1).start()
 
     q_second(1)
+    for i in range(2):
+        f_arrived(2, i)
+        f_pass(i).start()
     q_rest(1)
     prepare(1)
+    q_second(2)
+    q_second(3)
 
     @pl.when(middle)
     def _():
         m_arrived(near(3), far)
         m_pair(near(3), far, 1, 2).start()
-
-    q_second(2)
-    q_second(3)
-
-    @pl.when(middle)
-    def _():
         m_arrived(near(2), far)
         m_pair(near(2), far, 1, 3).start()
 
-    f_arrived(beside(2))
-    f_pass().start()
-    for t in (2, 3):
-        q_rest(t)
-        prepare(t)
+    for i in range(2, len(cuts)):
+        f_arrived(2, i)
+        f_pass(i).start()
     send(
         mt.at[j], mall.at[z, beside(1)], m_send.at[0, 0, 0], m_recv.at[z, y], z, beside(1)
     ).wait_recv()
     loads[7].wait()
-    f_arrived(beside(1))
-    f_arrived(beside(3))
     m_arrived(near(1), y)
     m_arrived(near(1), far)
-    early = (z, near(1))
+    for s in (1, 3):
+        for i in range(len(cuts)):
+            f_arrived(s, i)
+    for t in (2, 3):
+        q_rest(t)
+        prepare(t)
     gather(0, early)
-
-    def first_half(owner, carry):
-        acc[owner] = part(0, early, owner)
-        return carry
-
-    lax.fori_loop(0, 4, first_half, 0)
+    first_half(own_pair)
+    first_half(other_pair)
 
     @pl.when(jnp.logical_not(middle))
     def _():
@@ -497,19 +530,21 @@
         )
 
     group = iota((32, wide), 1) // 32
-    for t in (3, 2, 1, 0):
-        owner = near(t)
-        total = acc[owner] + part(1, late, owner)
-        total = total + pltpu.roll(total, wide // 2, 1)
-        total = total + pltpu.roll(total, wide // 4, 1)
-        total = total.reshape(4, 4, 32, wide)
-        packed = total[:, 3]
-        for b in (2, 1, 0):
-            packed = jnp.where(group == b, total[:, b], packed)
-        ret_out[owner] = packed.astype(BF)
-        for s in (3, 2, 1, 0):
-            if s or t:
-                ret_copy(t, s).start()
+    for ends, pair in (((3, 2), other_pair), ((1, 0), own_pair)):
+        total = (acc[pair] + part(1, late, pair)).reshape(8, 4, 32, wide)
+        packed = None
+        for k in range(4):
+            mixed = total[:, (3 - k) % 4]
+            for m in (2, 1, 0):
+                mixed = jnp.where(group == m, total[:, (m - k) % 4], mixed)
+            if k:
+                mixed = pltpu.roll(mixed, wide - 32 * k, 2)
+            packed = mixed if packed is None else packed + mixed
+        ret_out[pair] = packed.astype(BF).reshape(2, 4, 32, wide)
+        for t in ends:
+            for s in (3, 2, 1, 0):
+                if s or t:
+                    ret_copy(t, s).start()
     ret_in[j, z] = ret_out[z, j]
     for t in range(PLANES):
         for s in (0, 1, 2, 3):
@@ -550,9 +585,10 @@
         for to in (2, 1):
             q_pass(t, 0, to).wait_send()
         q_pass(t, 2, 1).wait_send()
-    for s in (2, 1):
-        f_copy(s).wait_send()
-    f_pass().wait_send()
+    for i in range(len(cuts)):
+        for s in (2, 1):
+            f_copy(s, i).wait_send()
+        f_pass(i).wait_send()
     for s in range(4):
         for t in range(PLANES):
             if s or t:
@@ -594,12 +630,12 @@
             pltpu.VMEM((PLANES, 4, rows, first_count * two), BF),
             pltpu.VMEM((wide, two + PLANES * wide), BF),
             pltpu.VMEM((PLANES, PLANES, 4 * pieces, wide), F32),
-            pltpu.VMEM((2, two, first_count * two), BF),
+            pltpu.VMEM((2, first_count * two, two), BF),
             pltpu.VMEM((PLANES, 4 * rows, wide), F32),
             pltpu.VMEM((4 * wide, PLANES * wide), BF),
             pltpu.VMEM((PLANES, 4, 32, wide), BF),
             pltpu.VMEM((4, PLANES, 32, wide), BF),
-            dma((8,)), dma((4, PLANES)), dma((PLANES, 4)), dma((3,)), dma((4,)),
+            dma((8,)), dma((4, PLANES)), dma((PLANES, 4)), dma((3, first_count)), dma((4, first_count)),
             dma((2, PLANES, 4)), dma((PLANES, 2)), dma((4, PLANES)), dma((4, PLANES)),
         ],
         compiler_params=pltpu.CompilerParams(

time: 32.4 us -> 30.7 us (0.948)
  Pallas kernels: 31.6 us -> 29.9 us
    pallas_call x1, Pallas kernels: 31.6 us -> 29.9 us  [on_device_planes(): pl.pallas_call(lambda *refs: planes_kernel(sizes, *refs), name='planes',...]
where the time goes in v3:
time: 30.7 us; the launch traced here: 30.6 us
  Pallas kernels  29.9 us (97%)
  local copies, waits for them, and re-layouts  0.63 us (2%)
    pallas_call x1, Pallas kernels, on_device_planes(): pl.pallas_call(lambda *refs: planes_kernel(sizes, *refs), name='planes',...  29.9 us
    unnamed x1, local copies, waits for them, and re-layouts  0.63 us

profile of v3, /device:TPU:0, one launch (start us, length us, event | category | flops | bytes accessed | tf_op | source)
XLA Modules:
  0.0 30.6 jit_solution(6784452841833473679)
XLA Ops:
  0.0 29.9 %planes.1 = f32[128,128]{1,0:T(8,128)S(1)} custom-call(bf16[64,1024]{1,0:T(8,128)(2,1)} %bitcast.9, s32[3,8]{1,0:T(4,128)} %bitcast.11, s32[3,8]{1,0:T(4,128)} %bitcast.12, s32[1,8]{1,0:T(1,128)} %bitcast.13, s32[8,12]{1,0:T(8,128)} %refs_4_.1, bf16[4,2,32,512]{3,2,1,0:T(8,128)(2,1)} %refs_5_.1, bf16[2,512,512]{2,1,0:T(8,128)(2,1)} %bitcast.8, ...), custom_call_target="tpu_custom_call" | custom-call | tf_op jit(solution)/shard_map/planes/pallas_call | solution.py:611
  30.0 0.6 %copy.10 = f32[8,16,128]{2,1,0:T(8,128)} copy(f32[8,16,128]{2,1,0:T(8,128)S(1)} %bitcast.7) | data formatting | bytes 131072

commit v4 on v3

--- a/solution.py
+++ b/solution.py
@@ -385,19 +385,16 @@
                     a * wide:(a + 1) * wide, r * two:(r + 1) * two
                 ]
 
-    own_pair = pl.ds(2 * (z // 2), 2)
-    other_pair = pl.ds(2 - 2 * (z // 2), 2)
-
-    def part(b, planes, pair):
-        lines = sel[pair].reshape(8 * rows, first_count * two)
+    def part(b, planes, owner):
+        lines = sel[owner].reshape(4 * rows, first_count * two)
         values = jnp.dot(lines, gall[b], preferred_element_type=F32)
         total = None
         for u, p in enumerate(planes):
-            mask = masks[p, pair].reshape(8 * pieces, 1, wide)
-            mask = jnp.broadcast_to(mask, (8 * pieces, rows_piece, wide))
-            term = values[:, u * wide:(u + 1) * wide] * mask.reshape(8 * rows, wide)
+            mask = masks[p, owner].reshape(4 * pieces, 1, wide)
+            mask = jnp.broadcast_to(mask, (4 * pieces, rows_piece, wide))
+            term = values[:, u * wide:(u + 1) * wide] * mask.reshape(4 * rows, wide)
             total = term if total is None else total + term
-        return total.reshape(2, 4 * rows, wide)
+        return total
 
     pl.semaphore_wait(barrier, 4 * PLANES - 1)
     far = flip(y, 1)
@@ -415,9 +412,6 @@
     def q_rest(t):
         q_arrived(t, 1)
         q_arrived(t, 3)
-
-    def first_half(pair):
-        acc[pair] = part(0, early, pair)
 
     edge = jnp.logical_not(middle)
     for s in (2, 3):
@@ -460,8 +454,6 @@
     f_copy(2, 1).start()
     q_second(0)
     q_spread(1)
-    for i in range(2, len(cuts)):
-        f_copy(2, i).start()
 
     @pl.when(middle)
     def _():
@@ -472,6 +464,8 @@
     prepare(0)
     q_spread(2)
     q_spread(3)
+    for i in range(2, len(cuts)):
+        f_copy(2, i).start()
 
     @pl.when(middle)
     def _():
@@ -479,14 +473,9 @@
         m_pair(near(2), y, 1, 1).start()
 
     q_second(1)
-    for i in range(2):
-        f_arrived(2, i)
-        f_pass(i).start()
-    q_rest(1)
-    prepare(1)
+    f_arrived(2, 0)
+    f_pass(0).start()
     q_second(2)
-    q_second(3)
-
     @pl.when(middle)
     def _():
         m_arrived(near(3), far)
@@ -494,9 +483,19 @@
         m_arrived(near(2), far)
         m_pair(near(2), far, 1, 3).start()
 
+    q_second(3)
+
+    f_arrived(2, 1)
+    f_pass(1).start()
+    q_rest(1)
+    prepare(1)
+    q_rest(2)
+    prepare(2)
     for i in range(2, len(cuts)):
         f_arrived(2, i)
         f_pass(i).start()
+    q_rest(3)
+    prepare(3)
     send(
         mt.at[j], mall.at[z, beside(1)], m_send.at[0, 0, 0], m_recv.at[z, y], z, beside(1)
     ).wait_recv()
@@ -506,12 +505,9 @@
     for s in (1, 3):
         for i in range(len(cuts)):
             f_arrived(s, i)
-    for t in (2, 3):
-        q_rest(t)
-        prepare(t)
     gather(0, early)
-    first_half(own_pair)
-    first_half(other_pair)
+    for t in (3, 2):
+        acc[near(t)] = part(0, early, near(t))
 
     @pl.when(jnp.logical_not(middle))
     def _():
@@ -530,17 +526,20 @@
         )
 
     group = iota((32, wide), 1) // 32
-    for ends, pair in (((3, 2), other_pair), ((1, 0), own_pair)):
-        total = (acc[pair] + part(1, late, pair)).reshape(8, 4, 32, wide)
-        packed = None
-        for k in range(4):
-            mixed = total[:, (3 - k) % 4]
-            for m in (2, 1, 0):
-                mixed = jnp.where(group == m, total[:, (m - k) % 4], mixed)
-            if k:
-                mixed = pltpu.roll(mixed, wide - 32 * k, 2)
-            packed = mixed if packed is None else packed + mixed
-        ret_out[pair] = packed.astype(BF).reshape(2, 4, 32, wide)
+    for ends in ((3, 2), (1, 0)):
+        for t in ends:
+            owner = near(t)
+            total = acc[owner] if t > 1 else part(0, early, owner)
+            total = (total + part(1, late, owner)).reshape(4, 4, 32, wide)
+            packed = None
+            for k in range(4):
+                mixed = total[:, (3 - k) % 4]
+                for m in (2, 1, 0):
+                    mixed = jnp.where(group == m, total[:, (m - k) % 4], mixed)
+                if k:
+                    mixed = pltpu.roll(mixed, wide - 32 * k, 2)
+                packed = mixed if packed is None else packed + mixed
+            ret_out[owner] = packed.astype(BF)
         for t in ends:
             for s in (3, 2, 1, 0):
                 if s or t:

time: 30.7 us -> 29.5 us (0.961)
  Pallas kernels: 29.9 us -> 28.7 us
    pallas_call x1, Pallas kernels: 29.9 us -> 28.7 us  [on_device_planes(): pl.pallas_call(lambda *refs: planes_kernel(sizes, *refs), name='planes',...]
where the time goes in v4:
time: 29.5 us; the launch traced here: 29.3 us
  Pallas kernels  28.7 us (97%)
  local copies, waits for them, and re-layouts  0.63 us (2%)
    pallas_call x1, Pallas kernels, on_device_planes(): pl.pallas_call(lambda *refs: planes_kernel(sizes, *refs), name='planes',...  28.7 us
    unnamed x1, local copies, waits for them, and re-layouts  0.63 us

profile of v4, /device:TPU:0, one launch (start us, length us, event | category | flops | bytes accessed | tf_op | source)
XLA Modules:
  0.0 29.3 jit_solution(11892634077180238587)
XLA Ops:
  0.0 28.7 %planes.1 = f32[128,128]{1,0:T(8,128)S(1)} custom-call(bf16[64,1024]{1,0:T(8,128)(2,1)} %bitcast.9, s32[3,8]{1,0:T(4,128)} %bitcast.11, s32[3,8]{1,0:T(4,128)} %bitcast.12, s32[1,8]{1,0:T(1,128)} %bitcast.13, s32[8,12]{1,0:T(8,128)} %refs_4_.1, bf16[4,2,32,512]{3,2,1,0:T(8,128)(2,1)} %refs_5_.1, bf16[2,512,512]{2,1,0:T(8,128)(2,1)} %bitcast.8, ...), custom_call_target="tpu_custom_call" | custom-call | tf_op jit(solution)/shard_map/planes/pallas_call | solution.py:610
  28.7 0.6 %copy.10 = f32[8,16,128]{2,1,0:T(8,128)} copy(f32[8,16,128]{2,1,0:T(8,128)S(1)} %bitcast.7) | data formatting | bytes 131072

commit v5 on v4

--- a/solution.py
+++ b/solution.py
@@ -342,7 +342,10 @@
         iota((rows_piece, two), 0) == iota((rows_piece, two), 1) % rows_piece, 1.0, 0.0
     ).astype(F32)
 
-    group_of = iota((rows, two), 1) // held_rows
+    group_of = [
+        jnp.where(iota((rows, two), 1) // held_rows == a, 1.0, 0.0).astype(BF)
+        for a in range(first_count)
+    ]
 
     def prepare(t):
         plane = near(t)
@@ -355,11 +358,8 @@
         for q in range(4):
             wanted = spread[q * pieces:(q + 1) * pieces, :two]
             kept = jnp.broadcast_to(wanted[:, None, :], (pieces, rows_piece, two)) * same[None]
-            kept = kept.reshape(rows, two)
-            left = jnp.concatenate(
-                [jnp.where(group_of == a, kept, 0.0).astype(BF) for a in range(first_count)],
-                axis=0,
-            )
+            kept = kept.reshape(rows, two).astype(BF)
+            left = jnp.concatenate([kept * group_of[a] for a in range(first_count)], axis=0)
             right = jnp.concatenate([qall[plane, q, :held_rows]] * first_count, axis=0)
             picked = jnp.dot(left, right, preferred_element_type=F32).astype(BF)
             for a in range(first_count):
@@ -430,9 +430,8 @@
 
     @pl.when(middle)
     def _():
-        for t in (1, 3):
-            for s in (0, 1):
-                m_near(t, s).start()
+        for s in (0, 1):
+            m_near(1, s).start()
 
     f_copy(2, 0).start()
     for i in range(len(cuts)):
@@ -457,8 +456,9 @@
 
     @pl.when(middle)
     def _():
-        for s in (0, 1):
-            m_near(2, s).start()
+        for t in (2, 3):
+            for s in (0, 1):
+                m_near(t, s).start()
 
     q_arrived(0, 3)
     prepare(0)
@@ -473,6 +473,12 @@
         m_pair(near(2), y, 1, 1).start()
 
     q_second(1)
+
+    @pl.when(middle)
+    def _():
+        m_arrived(near(2), far)
+        m_pair(near(2), far, 1, 3).start()
+
     f_arrived(2, 0)
     f_pass(0).start()
     q_second(2)
@@ -480,8 +486,6 @@
     def _():
         m_arrived(near(3), far)
         m_pair(near(3), far, 1, 2).start()
-        m_arrived(near(2), far)
-        m_pair(near(2), far, 1, 3).start()
 
     q_second(3)
 

time: 29.5 us -> 29.3 us (level)
  no operation moved by 1% of the time
where the time goes in v5:
time: 29.3 us; the launch traced here: 29.2 us
  Pallas kernels  28.5 us (97%)
  local copies, waits for them, and re-layouts  0.63 us (2%)
    pallas_call x1, Pallas kernels, on_device_planes(): pl.pallas_call(lambda *refs: planes_kernel(sizes, *refs), name='planes',...  28.5 us
    unnamed x1, local copies, waits for them, and re-layouts  0.63 us

profile of v5, /device:TPU:0, one launch (start us, length us, event | category | flops | bytes accessed | tf_op | source)
XLA Modules:
  0.0 29.2 jit_solution(6243114347290514305)
XLA Ops:
  0.0 28.5 %planes.1 = f32[128,128]{1,0:T(8,128)S(1)} custom-call(bf16[64,1024]{1,0:T(8,128)(2,1)} %bitcast.9, s32[3,8]{1,0:T(4,128)} %bitcast.11, s32[3,8]{1,0:T(4,128)} %bitcast.12, s32[1,8]{1,0:T(1,128)} %bitcast.13, s32[8,12]{1,0:T(8,128)} %refs_4_.1, bf16[4,2,32,512]{3,2,1,0:T(8,128)(2,1)} %refs_5_.1, bf16[2,512,512]{2,1,0:T(8,128)(2,1)} %bitcast.8, ...), custom_call_target="tpu_custom_call" | custom-call | tf_op jit(solution)/shard_map/planes/pallas_call | solution.py:614
  28.5 0.6 %copy.10 = f32[8,16,128]{2,1,0:T(8,128)} copy(f32[8,16,128]{2,1,0:T(8,128)S(1)} %bitcast.7) | data formatting | bytes 131072

commit v6 on v5

--- a/solution.py
+++ b/solution.py
@@ -478,15 +478,12 @@
     def _():
         m_arrived(near(2), far)
         m_pair(near(2), far, 1, 3).start()
+        m_arrived(near(3), far)
+        m_pair(near(3), far, 1, 2).start()
 
     f_arrived(2, 0)
     f_pass(0).start()
     q_second(2)
-    @pl.when(middle)
-    def _():
-        m_arrived(near(3), far)
-        m_pair(near(3), far, 1, 2).start()
-
     q_second(3)
 
     f_arrived(2, 1)

time: 29.3 us -> 29.3 us (level)
  no operation moved by 1% of the time
where the time goes in v6:
time: 29.3 us; the launch traced here: 29.2 us
  Pallas kernels  28.5 us (97%)
  local copies, waits for them, and re-layouts  0.63 us (2%)
    pallas_call x1, Pallas kernels, on_device_planes(): pl.pallas_call(lambda *refs: planes_kernel(sizes, *refs), name='planes',...  28.5 us
    unnamed x1, local copies, waits for them, and re-layouts  0.63 us

profile of v6, /device:TPU:0, one launch (start us, length us, event | category | flops | bytes accessed | tf_op | source)
XLA Modules:
  0.0 29.2 jit_solution(2793726383909074846)
XLA Ops:
  0.0 28.5 %planes.1 = f32[128,128]{1,0:T(8,128)S(1)} custom-call(bf16[64,1024]{1,0:T(8,128)(2,1)} %bitcast.9, s32[3,8]{1,0:T(4,128)} %bitcast.11, s32[3,8]{1,0:T(4,128)} %bitcast.12, s32[1,8]{1,0:T(1,128)} %bitcast.13, s32[8,12]{1,0:T(8,128)} %refs_4_.1, bf16[4,2,32,512]{3,2,1,0:T(8,128)(2,1)} %refs_5_.1, bf16[2,512,512]{2,1,0:T(8,128)(2,1)} %bitcast.8, ...), custom_call_target="tpu_custom_call" | custom-call | tf_op jit(solution)/shard_map/planes/pallas_call | solution.py:611
  28.5 0.6 %copy.10 = f32[8,16,128]{2,1,0:T(8,128)} copy(f32[8,16,128]{2,1,0:T(8,128)S(1)} %bitcast.7) | data formatting | bytes 131072
